TPU v7x, 32 devices: a whole 2x2x4 slice. The times are simulated.
32 devices in a mesh: segment: 2 (over y), frame: 16 (over z, x, core).
Axes of the slice: x: 2, y: 2, z: 4, core: 2. Of those that a mesh axis runs over, the one named last changes fastest.
Arguments:
- noisy_clips: bfloat16 [4, 16, 16, 16, 512], P(None, 'frame'), may hold values from -6 to 6
- conv_first: bfloat16 [2, 9, 512, 512], P('segment', None, 'frame'), may hold values from -0.09375 to 0.09375
- conv_second: bfloat16 [2, 9, 512, 512], P('segment', None, 'frame'), may hold values from -0.09375 to 0.09375
- temporal: bfloat16 [2, 3, 512, 512], P('segment', None, 'frame'), may hold values from -0.15625 to 0.15625
Outputs:
- denoised: bfloat16 [4, 16, 16, 16, 512], P(None, 'frame', 'segment')
All inputs are finite; a program needn't handle non-finite values.
Results may differ from a plain program's by a relative error of at most 0.013.
Values may be sent and summed in bfloat16 or wider, within the bound.
A program may use at most 64 MiB of HBM per device.

v0:
```python
import functools

import jax
import jax.numpy as jnp
from jax import lax
from jax.experimental import pallas as pl
from jax.experimental.pallas import tpu as pltpu
from jax.sharding import PartitionSpec as P

skip_scale = 0.7071067811865476
MESH = pl.DeviceIdType.MESH


def passed_along(shard, axis, by):
    length = lax.axis_size(axis)
    pairs = [(i, i + by) for i in range(length) if 0 <= i + by < length]
    return lax.ppermute(shard, axis, pairs)


def extended_2(cells, sides, width):
    for axis, dim in sides:
        count = lax.axis_size(axis)
        ends = count - 1
        head = lax.slice_in_dim(cells, 0, width, axis=dim)
        tail = lax.slice_in_dim(cells, cells.shape[dim] - width, cells.shape[dim], axis=dim)
        cells = jnp.concatenate(
            [
                lax.ppermute(tail, axis, [(i, (i + 1) % count) for i in range(ends)]),
                cells,
                lax.ppermute(head, axis, [((i + 1) % count, i) for i in range(ends)]),
            ],
            axis=dim,
        )
    return cells


def broadcast(shard, axis, root):
    mine = lax.axis_index(axis) == root
    return lax.psum(jnp.where(mine, shard, jnp.zeros_like(shard)), axis)


def spatial(field_in, kernel):
    extent = field_in.shape[1]
    channels = field_in.shape[3]
    padded = jnp.pad(field_in, ((0, 0), (1, 1), (1, 1), (0, 0)))
    accumulated = jnp.zeros((field_in.shape[0] * extent * extent, channels), jnp.float32)
    for row_shift in range(3):
        for col_shift in range(3):
            window = padded[
                :, row_shift : row_shift + extent, col_shift : col_shift + extent, :
            ].reshape(-1, channels)
            accumulated = accumulated + jnp.dot(
                window, kernel[3 * row_shift + col_shift], preferred_element_type=jnp.float32
            )
    return accumulated.reshape(field_in.shape)


def temporal_mix(extended, kernel, frame_local):
    channels = extended.shape[3]
    out_shape = (frame_local,) + extended.shape[1:]
    accumulated = jnp.zeros(out_shape, jnp.float32)
    for offset in range(3):
        window = extended[offset : offset + frame_local].reshape(-1, channels)
        accumulated = accumulated + jnp.dot(
            window, kernel[offset], preferred_element_type=jnp.float32
        ).reshape(out_shape)
    return accumulated


def pipelined(noisy_clips, conv_first, conv_second, temporal):
    sections = lax.axis_size("segment")
    segment_id = lax.axis_index("segment")
    first_full, second_full, time_full = (
        lax.all_gather(conv_first, "frame", axis=2, tiled=True),
        lax.all_gather(conv_second, "frame", axis=2, tiled=True),
        lax.all_gather(temporal, "frame", axis=2, tiled=True),
    )
    first_kernel = first_full[0]
    second_kernel = second_full[0]
    time_kernel = time_full[0]
    clip_count = noisy_clips.shape[0]
    frame_local = noisy_clips.shape[1]
    side_len = noisy_clips.shape[2]
    block_shape = noisy_clips.shape[1:]
    tick_count = clip_count + sections - 1
    half_sections = sections // 2
    is_up = segment_id >= half_sections
    store_depth = max(half_sections - 1, 1)
    side_store = jnp.zeros((store_depth,) + block_shape, jnp.bfloat16)
    out_store = jnp.zeros(noisy_clips.shape, jnp.bfloat16)
    prev_out = jnp.zeros(block_shape, jnp.bfloat16)

    def tick_step(carry, tick_index):
        prev_out, side_store, out_store = carry
        clip_now = tick_index - segment_id
        active = (clip_now >= 0) & (clip_now < clip_count)
        clip_slot = jnp.clip(clip_now, 0, clip_count - 1)
        own_input = lax.dynamic_index_in_dim(noisy_clips, clip_slot, 0, keepdims=False)
        received, side_store = passed_along((prev_out, side_store), "segment", 1)
        entering = jnp.where(segment_id == 0, own_input, received)
        written = (jnp.arange(store_depth) == segment_id - 1) & (segment_id < half_sections)
        side_store = jnp.where(written[:, None, None, None, None], entering[None], side_store)
        stack_slot = jnp.clip(sections - 2 - segment_id, 0, store_depth - 1)
        stored = lax.dynamic_index_in_dim(side_store, stack_slot, 0, keepdims=False)
        skip_feature = jnp.where(segment_id == sections - 1, own_input, stored)
        joined = (
            (entering.astype(jnp.float32) + skip_feature.astype(jnp.float32)) * skip_scale
        ).astype(jnp.bfloat16)
        section_in = jnp.where(is_up, joined, entering)
        activated = lax.cond(
            active,
            lambda: jax.nn.silu(spatial(section_in, first_kernel)).astype(jnp.bfloat16),
            lambda: jnp.zeros(block_shape, jnp.bfloat16),
        )
        extended = extended_2(activated, (("frame", 0),), 1)

        def second_pass():
            branch_sum = spatial(activated, second_kernel) + temporal_mix(
                extended, time_kernel, frame_local
            )
            return (section_in.astype(jnp.float32) + jax.nn.silu(branch_sum)).astype(jnp.bfloat16)

        section_out = lax.cond(active, second_pass, lambda: jnp.zeros(block_shape, jnp.bfloat16))
        finished = (jnp.arange(clip_count) == clip_slot) & active & (segment_id == sections - 1)
        out_store = jnp.where(finished[:, None, None, None, None], section_out[None], out_store)
        return ((section_out, side_store, out_store), None)

    final_carry, unused = lax.scan(
        tick_step, (prev_out, side_store, out_store), jnp.arange(tick_count, dtype=jnp.int32)
    )
    delivered = broadcast(final_carry[2], "segment", sections - 1)
    slab_rows = side_len // sections
    return lax.dynamic_slice_in_dim(delivered, segment_id * slab_rows, slab_rows, 2)


def fused_kernel(
    frames,
    noisy_ref,
    first_ref,
    second_ref,
    time_ref,
    out_ref,
    w_ref,
    xe,
    xa,
    a_send,
    a_recv,
    t_send,
    t_recv,
    e_mine,
    e_recv,
    acc_ref,
    o_full,
    o_take,
    local_sem,
    y_sems,
    ring_sems,
    pair_sems,
    a_sems,
    t_sems,
    e_sems,
    o_sems,
):
    clips, side, lanes = noisy_ref.shape[0], noisy_ref.shape[2], noisy_ref.shape[4]
    half = lanes // 2
    cells = side * side
    depth = first_ref.shape[2]
    taps = first_ref.shape[1] + time_ref.shape[1] + second_ref.shape[1]
    n = frames // 2
    seg = lax.axis_index("segment")
    me = lax.axis_index("frame")
    core, chip = lax.rem(me, 2), me // 2
    peer = 1 - seg
    other = chip * 2 + (1 - core)

    def frame_at(place):
        place = lax.rem(place + 2 * n, n)
        return jnp.where(place < n // 2, 2 * place, 2 * (n - 1 - place) + 1) * 2 + core

    pos = jnp.where(lax.rem(chip, 2) == 0, chip // 2, n - 1 - chip // 2)
    right, left = frame_at(pos + 1), frame_at(pos - 1)
    after, before = lax.rem(me + 1, frames), lax.rem(me + frames - 1, frames)

    barrier = pltpu.get_barrier_semaphore()
    pl.semaphore_signal(barrier, inc=1, device_id=(peer, me), device_id_type=MESH)
    for target in (right, left, other, after, before):
        pl.semaphore_signal(barrier, inc=1, device_id=(seg, target), device_id_type=MESH)
    pl.semaphore_wait(barrier, 6)

    def columns(which):
        return pl.ds(pl.multiple_of(which * half, half), half)

    parts = ((first_ref, 0, 9), (time_ref, 9, 3), (second_ref, 12, 9))
    own_rows = pl.ds(pl.multiple_of(me * depth, depth), depth)

    def local_copy(i):
        ref, start, count = parts[i]
        return pltpu.make_async_copy(
            ref.at[0, :, :, columns(seg)],
            w_ref.at[pl.ds(seg * taps + start, count), own_rows],
            local_sem.at[i],
        )

    def remote(src, dst, sems, index, device):
        return pltpu.make_async_remote_copy(
            src_ref=src,
            dst_ref=dst,
            send_sem=sems.at[(0,) + index],
            recv_sem=sems.at[(1,) + index],
            device_id=device,
            device_id_type=MESH,
        )

    def y_copy(i):
        ref, start, count = parts[i]
        return remote(
            ref.at[0, :, :, columns(peer)],
            w_ref.at[pl.ds(seg * taps + start, count), own_rows],
            y_sems,
            (i,),
            (peer, me),
        )

    for i in range(3):
        y_copy(i).start()
        local_copy(i).start()

    groups = (
        (0, (0,), ((0, 5), (5, 4))),
        (0, (1, 2), ((9, 6), (15, 6))),
        (1, (0,), ((0, 5), (5, 4))),
        (1, (1, 2), ((9, 6), (15, 6))),
    )
    streams = tuple((way, sub) for sub in range(2) for way in range(2))
    mid = depth // 2

    def slab(g, q, step):
        section, _, subs = groups[g]
        way, sub = streams[q]
        start, count = subs[sub]
        owner = frame_at(pos - step if way == 0 else pos + step)
        rows = pl.ds(pl.multiple_of(owner * depth + way * mid, mid), mid)
        return w_ref.at[pl.ds(section * taps + start, count), rows]

    def ring(g, q, step):
        ref = slab(g, q, step)
        return remote(ref, ref, ring_sems, (g, q, step), (seg, right if streams[q][0] == 0 else left))

    def paired(g, q, step):
        ref = slab(g, q, step)
        return remote(ref, ref, pair_sems, (g, q, step), (seg, other))

    every = range(len(streams))

    def begin(g):
        section, needed, _ = groups[g]

        @pl.when(seg == section)
        def _():
            for i in needed:
                local_copy(i).wait()

        @pl.when(seg != section)
        def _():
            for i in needed:
                y_copy(i).wait_recv()

        for q in every:
            ring(g, q, 0).start()
            paired(g, q, 0).start()

    def advance(g, step):
        for q in every:
            ring(g, q, step - 1).wait_recv()

            @pl.when(step < n - 1)
            def _():
                ring(g, q, step).start()

            paired(g, q, step).start()

    def complete(g):
        @pl.loop(0, n)
        def _(step):
            for q in every:
                paired(g, q, step).wait_recv()

    def build(x, clip, value, where):
        width = value.shape[1]
        wide = value.astype(jnp.float32)
        place = lax.broadcasted_iota(jnp.int32, (cells, width), 0) % side
        shifted = (
            jnp.where(place == 0, 0.0, pltpu.roll(wide, 1, 0)).astype(jnp.bfloat16),
            value,
            jnp.where(place == side - 1, 0.0, pltpu.roll(wide, cells - 1, 0)).astype(jnp.bfloat16),
        )
        for dx in range(3):
            x[dx, clip, 1 : side + 1, :, where] = shifted[dx].reshape(side, side, width)

    def spatial_sum(x, clip, base):
        total = None
        for dy in range(3):
            for dx in range(3):
                view = x[dx, clip, dy : dy + side].reshape(cells, lanes)
                term = jnp.dot(
                    view, w_ref[base + 3 * dy + dx], preferred_element_type=jnp.float32
                )
                total = term if total is None else total + term
        return total

    def silu(u):
        return u / (1.0 + jnp.exp(-u))

    def a_copy(s, clip):
        return remote(a_send.at[s, clip], a_recv.at[s, clip], a_sems, (s, clip), (peer, me))

    def e_copy(clip):
        return remote(e_mine.at[clip], e_recv.at[clip], e_sems, (clip,), (peer, me))

    def t_copy(s, way, clip):
        target = after if way == 0 else before
        return remote(
            t_send.at[s, way, clip], t_recv.at[s, way, clip], t_sems, (s, way, clip), (seg, target)
        )

    def first_conv(s, clip):
        total = spatial_sum(xe, clip, s * taps)
        a_send[s, clip] = silu(total).astype(jnp.bfloat16)
        a_copy(s, clip).start()

    def take_active(s, clip):
        a_copy(s, clip).wait_recv()
        build(xa, clip, a_send[s, clip], columns(seg))
        build(xa, clip, a_recv[s, clip], columns(peer))

    sends_on = (me < frames - 1, me > 0)
    takes_on = (me > 0, me < frames - 1)

    def mixed(s, clip, k):
        view = xa[1, clip, 1 : side + 1].reshape(cells, lanes)
        return jnp.dot(view, w_ref[s * taps + 9 + k], preferred_element_type=jnp.float32)

    def send_terms(s, clip):
        for way, k in ((0, 0), (1, 2)):
            t_send[s, way, clip] = mixed(s, clip, k).astype(jnp.bfloat16)

            @pl.when(sends_on[way])
            def _():
                t_copy(s, way, clip).start()

    def second_conv(s, clip):
        acc_ref[clip] = spatial_sum(xa, clip, s * taps + 12) + mixed(s, clip, 1)

    def finished(s, clip):
        for way in range(2):

            @pl.when(takes_on[way])
            def _():
                t_copy(s, way, clip).wait_recv()
                acc_ref[clip] = acc_ref[clip] + t_recv[s, way, clip].astype(jnp.float32)

        return silu(acc_ref[clip])

    def end_first(clip):
        own = noisy_ref[clip, 0, :, :, columns(seg)].reshape(cells, half).astype(jnp.float32)
        out = (own + finished(0, clip)).astype(jnp.bfloat16)
        e_mine[clip] = ((out.astype(jnp.float32) + own) * skip_scale).astype(jnp.bfloat16)
        e_copy(clip).start()

    def take_entering(clip):
        e_copy(clip).wait_recv()
        build(xe, clip, e_mine[clip], columns(seg))
        build(xe, clip, e_recv[clip], columns(peer))

    def end_second(clip):
        out = (e_mine[clip].astype(jnp.float32) + finished(1, clip)).astype(jnp.bfloat16)
        o_full[clip] = out.reshape(side, side, half)
        o_send(clip).start()

    def o_send(clip):
        slab_rows = side // 2
        return remote(
            o_full.at[clip, pl.ds(peer * slab_rows, slab_rows)],
            o_take.at[clip],
            o_sems,
            (clip,),
            (peer, me),
        )

    def staged(steps, plan):
        for offset, work in plan:

            @pl.when((steps >= offset) & (steps < offset + clips))
            def _():
                work(steps - offset)

    edge = jnp.zeros((side, lanes), jnp.bfloat16)
    for x in (xe, xa):
        for dx in range(3):

            @pl.loop(0, clips)
            def _(clip):
                x[dx, clip, 0] = edge
                x[dx, clip, side + 1] = edge

    def both(s):
        def work(clip):
            send_terms(s, clip)
            second_conv(s, clip)

        return work

    skew = n // 2 - 1
    ready = [g * skew + n for g in range(len(groups))]
    start_terms = max(ready[1], ready[0] + 4)
    start_next = max(ready[2], start_terms + 5)
    plan = (
        (0, lambda clip: build(xe, clip, noisy_ref[clip, 0].reshape(cells, lanes), slice(None))),
        (ready[0], lambda clip: first_conv(0, clip)),
        (start_terms - 1, lambda clip: take_active(0, clip)),
        (start_terms, both(0)),
        (start_terms + 2, end_first),
        (start_next - 1, take_entering),
        (start_next, lambda clip: first_conv(1, clip)),
        (start_next + 3, lambda clip: take_active(1, clip)),
    )
    last = max([ready[-1] + 1] + [offset + clips for offset, _ in plan])

    @pl.loop(0, last)
    def _(step):
        for g in range(len(groups)):

            @pl.when((step > g * skew) & (step < ready[g]))
            def _():
                advance(g, step - g * skew)

            @pl.when(step == g * skew)
            def _():
                begin(g)

            @pl.when(step == ready[g])
            def _():
                complete(g)

        staged(step, plan)

    @pl.loop(0, clips)
    def _(clip):
        send_terms(1, clip)

    @pl.loop(0, clips)
    def _(clip):
        second_conv(1, clip)
        end_second(clip)

    slab_rows = side // 2

    @pl.loop(0, clips)
    def _(clip):
        out_ref[clip, 0, :, :, columns(seg)] = o_full[clip, pl.ds(seg * slab_rows, slab_rows)]
        o_send(clip).wait_recv()
        out_ref[clip, 0, :, :, columns(peer)] = o_take[clip]
        o_send(clip).wait_send()
        e_copy(clip).wait_send()
        for s in range(2):
            a_copy(s, clip).wait_send()
            for way in range(2):

                @pl.when(sends_on[way])
                def _():
                    t_copy(s, way, clip).wait_send()

    for i in range(3):
        y_copy(i).wait_send()

    @pl.loop(0, n)
    def _(step):
        for g in range(len(groups)):
            for q in every:
                paired(g, q, step).wait_send()

                @pl.when(step < n - 1)
                def _():
                    ring(g, q, step).wait_send()


def on_device(noisy_clips, conv_first, conv_second, temporal):
    sections = lax.axis_size("segment")
    frames = lax.axis_size("frame")
    clips, frame_local, side, _, lanes = noisy_clips.shape
    half = lanes // 2
    cells = side * side
    if sections != 2 or half % 128 or frames % 4 or frames < 8 or frame_local != 1 or side % 16:
        return pipelined(noisy_clips, conv_first, conv_second, temporal)
    n = frames // 2
    dma = pltpu.SemaphoreType.DMA
    vmem = pl.BlockSpec(memory_space=pltpu.VMEM)
    kind = jnp.bfloat16
    return pl.pallas_call(
        functools.partial(fused_kernel, frames),
        out_shape=jax.ShapeDtypeStruct((clips, 1, side // 2, side, lanes), kind),
        in_specs=[vmem] * 4,
        out_specs=vmem,
        scratch_shapes=[
            pltpu.VMEM((42, lanes, half), kind),
            pltpu.VMEM((3, clips, side + 2, side, lanes), kind),
            pltpu.VMEM((3, clips, side + 2, side, lanes), kind),
            pltpu.VMEM((2, clips, cells, half), kind),
            pltpu.VMEM((2, clips, cells, half), kind),
            pltpu.VMEM((2, 2, clips, cells, half), kind),
            pltpu.VMEM((2, 2, clips, cells, half), kind),
            pltpu.VMEM((clips, cells, half), kind),
            pltpu.VMEM((clips, cells, half), kind),
            pltpu.VMEM((clips, cells, half), jnp.float32),
            pltpu.VMEM((clips, side, side, half), kind),
            pltpu.VMEM((clips, side // 2, side, half), kind),
            dma((3,)),
            dma((2, 3)),
            dma((2, 4, 4, n)),
            dma((2, 4, 4, n)),
            dma((2, 2, clips)),
            dma((2, 2, 2, clips)),
            dma((2, clips)),
            dma((2, clips)),
        ],
        compiler_params=pltpu.CompilerParams(
            collective_id=0, has_side_effects=True, vmem_limit_bytes=58 * 1024 * 1024
        ),
    )(noisy_clips, conv_first, conv_second, temporal)


def solution(mesh):
    in_specs = (
        P(None, "frame", None, None, None),
        P("segment", None, "frame", None),
        P("segment", None, "frame", None),
        P("segment", None, "frame", None),
    )
    out_specs = P(None, "frame", "segment", None, None)
    return jax.shard_map(
        on_device, mesh=mesh, in_specs=in_specs, out_specs=out_specs, check_vma=False
    )
```

profile of v0, /device:TPU:22, one launch (start us, length us, event | category | flops | bytes accessed | tf_op | source)
XLA Modules:
  0.0 119.0 jit_solution(16885489603237898504)
XLA Ops:
  0.0 117.1 %shard_map.46 = bf16[4,1,8,16,512]{4,3,2,1,0:T(8,128)(2,1)} custom-call(bf16[4,1,16,16,512]{4,3,2,1,0:T(8,128)(2,1)} %noisy_ref.1, bf16[1,9,32,512]{3,2,1,0:T(8,128)(2,1)} %first_ref.1, bf16[1,9,32,512]{3,2,1,0:T(8,128)(2,1)} %second_ref.1, bf16[1,3,32,512]{3,2,1,0:T(8,128)(2,1)} %time_ref.1), custom_call_target="tpu_custom_call" | custom-call | tf_op jit(solution)/shard_map/pallas_call | solution.py:499
  117.1 1.9 %copy.6 = bf16[4,1,8,16,512]{4,3,2,1,0:T(8,128)(2,1)} copy(bf16[4,1,8,16,512]{4,3,2,1,0:T(8,128)(2,1)} %shard_map.46) | data formatting | bytes 1048576
where the time goes:
time: 119 us
  Pallas kernels  117 us (98%)
  local copies, waits for them, and re-layouts  1.87 us (2%)
    pallas_call x1, Pallas kernels, on_device(): pl.pallas_call(functools.partial(fused_kernel, frames), out_shape=jax.Sha...  117 us

commit v1 on v0

v1 whole, which is shorter than its diff:
```python
import functools

import jax
import jax.numpy as jnp
from jax import lax
from jax.experimental import pallas as pl
from jax.experimental.pallas import tpu as pltpu
from jax.sharding import PartitionSpec as P

skip_scale = 0.7071067811865476
MESH = pl.DeviceIdType.MESH


def passed_along(shard, axis, by):
    length = lax.axis_size(axis)
    pairs = [(i, i + by) for i in range(length) if 0 <= i + by < length]
    return lax.ppermute(shard, axis, pairs)


def extended_2(cells, sides, width):
    for axis, dim in sides:
        count = lax.axis_size(axis)
        ends = count - 1
        head = lax.slice_in_dim(cells, 0, width, axis=dim)
        tail = lax.slice_in_dim(cells, cells.shape[dim] - width, cells.shape[dim], axis=dim)
        cells = jnp.concatenate(
            [
                lax.ppermute(tail, axis, [(i, (i + 1) % count) for i in range(ends)]),
                cells,
                lax.ppermute(head, axis, [((i + 1) % count, i) for i in range(ends)]),
            ],
            axis=dim,
        )
    return cells


def broadcast(shard, axis, root):
    mine = lax.axis_index(axis) == root
    return lax.psum(jnp.where(mine, shard, jnp.zeros_like(shard)), axis)


def spatial(field_in, kernel):
    extent = field_in.shape[1]
    channels = field_in.shape[3]
    padded = jnp.pad(field_in, ((0, 0), (1, 1), (1, 1), (0, 0)))
    accumulated = jnp.zeros((field_in.shape[0] * extent * extent, channels), jnp.float32)
    for row_shift in range(3):
        for col_shift in range(3):
            window = padded[
                :, row_shift : row_shift + extent, col_shift : col_shift + extent, :
            ].reshape(-1, channels)
            accumulated = accumulated + jnp.dot(
                window, kernel[3 * row_shift + col_shift], preferred_element_type=jnp.float32
            )
    return accumulated.reshape(field_in.shape)


def temporal_mix(extended, kernel, frame_local):
    channels = extended.shape[3]
    out_shape = (frame_local,) + extended.shape[1:]
    accumulated = jnp.zeros(out_shape, jnp.float32)
    for offset in range(3):
        window = extended[offset : offset + frame_local].reshape(-1, channels)
        accumulated = accumulated + jnp.dot(
            window, kernel[offset], preferred_element_type=jnp.float32
        ).reshape(out_shape)
    return accumulated


def pipelined(noisy_clips, conv_first, conv_second, temporal):
    sections = lax.axis_size("segment")
    segment_id = lax.axis_index("segment")
    first_full, second_full, time_full = (
        lax.all_gather(conv_first, "frame", axis=2, tiled=True),
        lax.all_gather(conv_second, "frame", axis=2, tiled=True),
        lax.all_gather(temporal, "frame", axis=2, tiled=True),
    )
    first_kernel = first_full[0]
    second_kernel = second_full[0]
    time_kernel = time_full[0]
    clip_count = noisy_clips.shape[0]
    frame_local = noisy_clips.shape[1]
    side_len = noisy_clips.shape[2]
    block_shape = noisy_clips.shape[1:]
    tick_count = clip_count + sections - 1
    half_sections = sections // 2
    is_up = segment_id >= half_sections
    store_depth = max(half_sections - 1, 1)
    side_store = jnp.zeros((store_depth,) + block_shape, jnp.bfloat16)
    out_store = jnp.zeros(noisy_clips.shape, jnp.bfloat16)
    prev_out = jnp.zeros(block_shape, jnp.bfloat16)

    def tick_step(carry, tick_index):
        prev_out, side_store, out_store = carry
        clip_now = tick_index - segment_id
        active = (clip_now >= 0) & (clip_now < clip_count)
        clip_slot = jnp.clip(clip_now, 0, clip_count - 1)
        own_input = lax.dynamic_index_in_dim(noisy_clips, clip_slot, 0, keepdims=False)
        received, side_store = passed_along((prev_out, side_store), "segment", 1)
        entering = jnp.where(segment_id == 0, own_input, received)
        written = (jnp.arange(store_depth) == segment_id - 1) & (segment_id < half_sections)
        side_store = jnp.where(written[:, None, None, None, None], entering[None], side_store)
        stack_slot = jnp.clip(sections - 2 - segment_id, 0, store_depth - 1)
        stored = lax.dynamic_index_in_dim(side_store, stack_slot, 0, keepdims=False)
        skip_feature = jnp.where(segment_id == sections - 1, own_input, stored)
        joined = (
            (entering.astype(jnp.float32) + skip_feature.astype(jnp.float32)) * skip_scale
        ).astype(jnp.bfloat16)
        section_in = jnp.where(is_up, joined, entering)
        activated = lax.cond(
            active,
            lambda: jax.nn.silu(spatial(section_in, first_kernel)).astype(jnp.bfloat16),
            lambda: jnp.zeros(block_shape, jnp.bfloat16),
        )
        extended = extended_2(activated, (("frame", 0),), 1)

        def second_pass():
            branch_sum = spatial(activated, second_kernel) + temporal_mix(
                extended, time_kernel, frame_local
            )
            return (section_in.astype(jnp.float32) + jax.nn.silu(branch_sum)).astype(jnp.bfloat16)

        section_out = lax.cond(active, second_pass, lambda: jnp.zeros(block_shape, jnp.bfloat16))
        finished = (jnp.arange(clip_count) == clip_slot) & active & (segment_id == sections - 1)
        out_store = jnp.where(finished[:, None, None, None, None], section_out[None], out_store)
        return ((section_out, side_store, out_store), None)

    final_carry, unused = lax.scan(
        tick_step, (prev_out, side_store, out_store), jnp.arange(tick_count, dtype=jnp.int32)
    )
    delivered = broadcast(final_carry[2], "segment", sections - 1)
    slab_rows = side_len // sections
    return lax.dynamic_slice_in_dim(delivered, segment_id * slab_rows, slab_rows, 2)


def fused_kernel(
    frames,
    noisy_ref,
    first_ref,
    second_ref,
    time_ref,
    out_ref,
    w_ref,
    xe,
    xa,
    a_send,
    a_recv,
    t_send,
    t_recv,
    e_mine,
    e_recv,
    acc_ref,
    o_full,
    local_sem,
    y_sem,
    got_sem,
    sent_sem,
    a_sem,
    t_sem,
    e_sem,
    o_sem,
):
    clips, side, lanes = noisy_ref.shape[0], noisy_ref.shape[2], noisy_ref.shape[4]
    half = lanes // 2
    cells = side * side
    depth = first_ref.shape[2]
    width = time_ref.shape[1]
    rows_per_conv = first_ref.shape[1] // width
    per_section = 2 * rows_per_conv + 1
    taps = per_section * width
    groups = 2 * per_section
    line = frames // 4
    seg = lax.axis_index("segment")
    me = lax.axis_index("frame")
    core, x_at, z_at = lax.rem(me, 2), lax.rem(me // 2, 2), me // 4
    peer = 1 - seg
    other = me + 1 - 2 * core
    slab_rows = side // 2

    def frame_of(x_place, z_place):
        return (z_place * 2 + x_place) * 2 + core

    x_peer = frame_of(1 - x_at, z_at)
    z_pair = z_at + 1 - 2 * lax.rem(z_at, 2)
    z_half = z_at // 2
    far = []
    for k in range(1, line // 2):
        part = lax.rem(z_half + k, line // 2)
        far += [2 * part, 2 * part + 1]
    after, before = lax.rem(me + 1, frames), lax.rem(me + frames - 1, frames)

    barrier = pltpu.get_barrier_semaphore()
    pl.semaphore_signal(barrier, inc=1, device_id=(peer, me), device_id_type=MESH)
    near = [other, x_peer, after, before] + [frame_of(x_at, z) for z in far + [z_pair]]
    for target in near:
        pl.semaphore_signal(barrier, inc=1, device_id=(seg, target), device_id_type=MESH)

    def columns(which):
        return pl.ds(pl.multiple_of(which * half, half), half)

    def rows_of(owner):
        return pl.ds(pl.multiple_of(owner * depth, depth), depth)

    def part(j):
        if j < rows_per_conv:
            return first_ref, j * width
        if j == rows_per_conv:
            return time_ref, 0
        return second_ref, (j - rows_per_conv - 1) * width

    def local_copy(j):
        ref, start = part(j)
        return pltpu.make_async_copy(
            ref.at[0, pl.ds(start, width), :, columns(seg)],
            w_ref.at[pl.ds(seg * taps + j * width, width), rows_of(me)],
            local_sem.at[j],
        )

    def remote(src, dst, send, recv, device):
        return pltpu.make_async_remote_copy(
            src_ref=src,
            dst_ref=dst,
            send_sem=send,
            recv_sem=recv,
            device_id=device,
            device_id_type=MESH,
        )

    def take(ref, sem):
        pltpu.make_async_copy(ref, ref, sem).wait()

    def y_copy(j):
        ref, start = part(j)
        return remote(
            ref.at[0, pl.ds(start, width), :, columns(peer)],
            w_ref.at[pl.ds(seg * taps + j * width, width), rows_of(me)],
            y_sem.at[per_section],
            y_sem.at[j],
            (peer, me),
        )

    def slab(g, owner):
        return w_ref.at[pl.ds(g * width, width), rows_of(owner)]

    def some(g, count):
        return w_ref.at[pl.ds(g * width, width), pl.ds(0, count * depth)]

    own, crossed, lined, rest = 0, 1, 2, 3

    def give(g, owner, kind, link, target):
        ref = slab(g, owner)
        remote(ref, ref, sent_sem.at[link], got_sem.at[kind, g], (seg, target)).start()

    def give_core(g, owner):
        give(g, owner, own, 2, other)

    def round_own(g):
        section, j = g // per_section, lax.rem(g, per_section)

        @pl.when(seg == section)
        def _():
            take(slab(g, me), local_sem.at[j])

        @pl.when(seg != section)
        def _():
            take(slab(g, me), y_sem.at[j])

        give(g, me, crossed, 0, x_peer)
        for z in far:
            give(g, me, lined, 1, frame_of(x_at, z))
        give(g, me, rest, 1, frame_of(x_at, z_pair))
        give_core(g, me)

    def round_cross(g):
        take(some(g, 1), got_sem.at[crossed, g])
        give(g, x_peer, rest, 1, frame_of(x_at, z_pair))
        give_core(g, x_peer)

    def round_line(g):
        take(some(g, len(far)), got_sem.at[lined, g])
        for z in far:
            give(g, frame_of(x_at, z), rest, 0, x_peer)
        for z in far:
            give_core(g, frame_of(x_at, z))

    def round_rest(g):
        take(some(g, len(far) + 2), got_sem.at[rest, g])
        give_core(g, frame_of(x_at, z_pair))
        give_core(g, frame_of(1 - x_at, z_pair))
        for z in far:
            give_core(g, frame_of(1 - x_at, z))

    def round_done(g):
        take(some(g, 2 * line), got_sem.at[own, g])

    def build(x, clip, value, where):
        width_of = value.shape[1]
        wide = value.astype(jnp.float32)
        place = lax.broadcasted_iota(jnp.int32, (cells, width_of), 0) % side
        shifted = (
            jnp.where(place == 0, 0.0, pltpu.roll(wide, 1, 0)).astype(jnp.bfloat16),
            value,
            jnp.where(place == side - 1, 0.0, pltpu.roll(wide, cells - 1, 0)).astype(jnp.bfloat16),
        )
        for dx in range(3):
            x[dx, clip, 1 : side + 1, :, where] = shifted[dx].reshape(side, side, width_of)

    def row_sum(x, clip, dy, base):
        total = None
        for dx in range(3):
            view = x[dx, clip, dy : dy + side].reshape(cells, lanes)
            term = jnp.dot(view, w_ref[base + dx], preferred_element_type=jnp.float32)
            total = term if total is None else total + term
        return total

    def silu(u):
        return u / (1.0 + jnp.exp(-u))

    def a_copy(s, clip):
        return remote(
            a_send.at[s, clip], a_recv.at[s, clip], a_sem.at[2, 0], a_sem.at[s, clip], (peer, me)
        )

    def e_copy(clip):
        return remote(e_mine.at[clip], e_recv.at[clip], e_sem.at[1, 0], e_sem.at[0, clip], (peer, me))

    def t_copy(s, way, clip):
        target = after if way == 0 else before
        return remote(
            t_send.at[way, s, clip],
            t_recv.at[way, s, clip],
            t_sem.at[way, 2, 0],
            t_sem.at[way, s, clip],
            (seg, target),
        )

    def o_copy(clip):
        return remote(
            o_full.at[clip, pl.ds(peer * slab_rows, slab_rows)],
            out_ref.at[clip, 0, :, :, columns(seg)],
            o_sem.at[1, 0],
            o_sem.at[0, clip],
            (peer, me),
        )

    def first_row(s, dy):
        def work(clip):
            term = row_sum(xe, clip, dy, s * taps + dy * width)
            acc_ref[clip] = term if dy == 0 else acc_ref[clip] + term

        return work

    def send_active(s):
        def work(clip):
            a_send[s, clip] = silu(acc_ref[clip]).astype(jnp.bfloat16)
            a_copy(s, clip).start()

        return work

    def take_active(s):
        def work(clip):
            a_copy(s, clip).wait_recv()
            build(xa, clip, a_send[s, clip], columns(seg))
            build(xa, clip, a_recv[s, clip], columns(peer))

        return work

    sends_on = (me < frames - 1, me > 0)
    takes_on = (me > 0, me < frames - 1)

    def terms(s):
        def work(clip):
            base = s * taps + rows_per_conv * width
            view = xa[1, clip, 1 : side + 1].reshape(cells, lanes)

            def mixed(k):
                return jnp.dot(view, w_ref[base + k], preferred_element_type=jnp.float32)

            for way, k in ((0, 0), (1, 2)):
                t_send[way, s, clip] = mixed(k).astype(jnp.bfloat16)

                @pl.when(sends_on[way])
                def _():
                    t_copy(s, way, clip).start()

            acc_ref[clip] = mixed(1)

        return work

    def second_row(s, dy):
        def work(clip):
            base = s * taps + (rows_per_conv + 1 + dy) * width
            acc_ref[clip] = acc_ref[clip] + row_sum(xa, clip, dy, base)

        return work

    def finished(s, clip):
        for way in range(2):

            @pl.when(takes_on[way])
            def _():
                t_copy(s, way, clip).wait_recv()
                acc_ref[clip] = acc_ref[clip] + t_recv[way, s, clip].astype(jnp.float32)

        return silu(acc_ref[clip])

    def end_first(clip):
        mine = noisy_ref[clip, 0, :, :, columns(seg)].reshape(cells, half).astype(jnp.float32)
        out = (mine + finished(0, clip)).astype(jnp.bfloat16)
        e_mine[clip] = ((out.astype(jnp.float32) + mine) * skip_scale).astype(jnp.bfloat16)
        e_copy(clip).start()

    def take_entering(clip):
        e_copy(clip).wait_recv()
        build(xe, clip, e_mine[clip], columns(seg))
        build(xe, clip, e_recv[clip], columns(peer))

    def end_second(clip):
        out = (e_mine[clip].astype(jnp.float32) + finished(1, clip)).astype(jnp.bfloat16)
        o_full[clip] = out.reshape(side, side, half)
        o_copy(clip).start()
        out_ref[clip, 0, :, :, columns(seg)] = o_full[clip, pl.ds(seg * slab_rows, slab_rows)]

    for j in range(per_section):
        local_copy(j).start()

    edge = jnp.zeros((side, lanes), jnp.bfloat16)
    for x in (xe, xa):
        for dx in range(3):

            @pl.loop(0, clips)
            def _(clip):
                x[dx, clip, 0] = edge
                x[dx, clip, side + 1] = edge

    @pl.loop(0, clips)
    def _(clip):
        build(xe, clip, noisy_ref[clip, 0].reshape(cells, lanes), slice(None))

    pl.semaphore_wait(barrier, len(near) + 1)

    for j in range(per_section):
        y_copy(j).start()

    beat = clips
    rounds = (
        (0, round_own),
        (3, round_cross),
        (5, round_line),
        (9, round_rest),
        (11, round_done),
    )

    def ready(g):
        return beat * g + rounds[-1][0]

    steps = (
        ((0, 1, ((0, 1), (0, 1), (0, 1))), (25, 3), (((27, 3), (31, 2), (36, 1)), (38, 1))),
        ((43, 3, ((43, 3), (44, 3), (47, 2))), (52, 3), (((56, 2), (60, 1), (63, 1)), (64, 1))),
    )
    plan = []
    for s in range(2):
        first, mixed_at, second = steps[s]
        base = per_section * s
        if s == 1:
            plan.append((first[0], first[1], take_entering))
        for dy, (offset, stride) in enumerate(first[2]):
            plan.append((max(offset, ready(base + dy)), stride, first_row(s, dy)))
        plan.append((plan[-1][0], plan[-1][1], send_active(s)))
        plan.append((mixed_at[0], mixed_at[1], take_active(s)))
        plan.append((max(mixed_at[0], ready(base + 3)), mixed_at[1], terms(s)))
        for dy, (offset, stride) in enumerate(second[0]):
            plan.append((max(offset, ready(base + 4 + dy)), stride, second_row(s, dy)))
        plan.append((second[1][0], second[1][1], end_first if s == 0 else end_second))
    last = max(offset + stride * (clips - 1) + 1 for offset, stride, _ in plan)

    @pl.loop(0, last)
    def _(step):
        for lag, work in reversed(rounds):
            at = step - lag

            @pl.when((at >= 0) & (lax.rem(at, beat) == 0) & (at < beat * groups))
            def _():
                work(at // beat)

        for offset, stride, work in plan:
            at = step - offset

            @pl.when((at >= 0) & (lax.rem(at, stride) == 0) & (at < stride * clips))
            def _():
                work(at // stride)

    @pl.loop(0, clips)
    def _(clip):
        o_copy(clip).wait_recv()

    take(o_full.at[:, pl.ds(0, slab_rows)], o_sem.at[1, 0])
    take(e_mine, e_sem.at[1, 0])
    take(a_send, a_sem.at[2, 0])
    for way in range(2):

        @pl.when(sends_on[way])
        def _():
            take(t_send.at[way], t_sem.at[way, 2, 0])

    take(w_ref.at[pl.ds(0, taps), pl.ds(0, depth)], y_sem.at[per_section])
    for link, count in enumerate((line - 1, line, 2 * line)):
        take(w_ref.at[:, pl.ds(0, count * depth)], sent_sem.at[link])


def on_device(noisy_clips, conv_first, conv_second, temporal):
    sections = lax.axis_size("segment")
    frames = lax.axis_size("frame")
    clips, frame_local, side, _, lanes = noisy_clips.shape
    half = lanes // 2
    cells = side * side
    if sections != 2 or half % 128 or frames % 8 or frames < 16 or frame_local != 1 or side % 16:
        return pipelined(noisy_clips, conv_first, conv_second, temporal)
    taps = conv_first.shape[1] + temporal.shape[1] + conv_second.shape[1]
    per_section = taps // temporal.shape[1]
    dma = pltpu.SemaphoreType.DMA
    vmem = pl.BlockSpec(memory_space=pltpu.VMEM)
    kind = jnp.bfloat16
    return pl.pallas_call(
        functools.partial(fused_kernel, frames),
        out_shape=jax.ShapeDtypeStruct((clips, 1, side // 2, side, lanes), kind),
        in_specs=[vmem] + [pl.BlockSpec(memory_space=pl.ANY)] * 3,
        out_specs=vmem,
        scratch_shapes=[
            pltpu.VMEM((2 * taps, lanes, half), kind),
            pltpu.VMEM((3, clips, side + 2, side, lanes), kind),
            pltpu.VMEM((3, clips, side + 2, side, lanes), kind),
            pltpu.VMEM((2, clips, cells, half), kind),
            pltpu.VMEM((2, clips, cells, half), kind),
            pltpu.VMEM((2, 2, clips, cells, half), kind),
            pltpu.VMEM((2, 2, clips, cells, half), kind),
            pltpu.VMEM((clips, cells, half), kind),
            pltpu.VMEM((clips, cells, half), kind),
            pltpu.VMEM((clips, cells, half), jnp.float32),
            pltpu.VMEM((clips, side, side, half), kind),
            dma((per_section,)),
            dma((per_section + 1,)),
            dma((4, 2 * per_section)),
            dma((3,)),
            dma((3, clips)),
            dma((2, 3, clips)),
            dma((2, clips)),
            dma((2, clips)),
        ],
        compiler_params=pltpu.CompilerParams(
            collective_id=0, has_side_effects=True, vmem_limit_bytes=58 * 1024 * 1024
        ),
    )(noisy_clips, conv_first, conv_second, temporal)


def solution(mesh):
    in_specs = (
        P(None, "frame", None, None, None),
        P("segment", None, "frame", None),
        P("segment", None, "frame", None),
        P("segment", None, "frame", None),
    )
    out_specs = P(None, "frame", "segment", None, None)
    return jax.shard_map(
        on_device, mesh=mesh, in_specs=in_specs, out_specs=out_specs, check_vma=False
    )
```

time: 119 us -> 103 us (0.87)
  the two profiles are of different devices: /device:TPU:22 before, /device:TPU:28 now
where the time goes in v1:
time: 103 us
  Pallas kernels  101 us (98%)
  local copies, waits for them, and re-layouts  1.87 us (2%)
    pallas_call x1, Pallas kernels, on_device(): pl.pallas_call(functools.partial(fused_kernel, frames), out_shape=jax.Sha...  101 us

profile of v1, /device:TPU:28, one launch (start us, length us, event | category | flops | bytes accessed | tf_op | source)
XLA Modules:
  0.0 102.8 jit_solution(2353715722338079996)
XLA Ops:
  0.0 101.0 %shard_map.46 = bf16[4,1,8,16,512]{4,3,2,1,0:T(8,128)(2,1)} custom-call(bf16[4,1,16,16,512]{4,3,2,1,0:T(8,128)(2,1)} %noisy_ref.1, bf16[1,9,32,512]{3,2,1,0:T(8,128)(2,1)} %first_ref.1, bf16[1,9,32,512]{3,2,1,0:T(8,128)(2,1)} %second_ref.1, bf16[1,3,32,512]{3,2,1,0:T(8,128)(2,1)} %time_ref.1), custom_call_target="tpu_custom_call" | custom-call | tf_op jit(solution)/shard_map/pallas_call | solution.py:524
  101.0 1.9 %copy.6 = bf16[4,1,8,16,512]{4,3,2,1,0:T(8,128)(2,1)} copy(bf16[4,1,8,16,512]{4,3,2,1,0:T(8,128)(2,1)} %shard_map.46) | data formatting | bytes 1048576

commit v2 on v1

--- a/solution.py
+++ b/solution.py
@@ -141,6 +141,7 @@
     time_ref,
     out_ref,
     w_ref,
+    n_ref,
     xe,
     xa,
     a_send,
@@ -152,6 +153,7 @@
     acc_ref,
     o_full,
     local_sem,
+    n_sem,
     y_sem,
     got_sem,
     sent_sem,
@@ -172,7 +174,8 @@
     line = frames // 4
     seg = lax.axis_index("segment")
     me = lax.axis_index("frame")
-    core, x_at, z_at = lax.rem(me, 2), lax.rem(me // 2, 2), me // 4
+    slots = frames // line
+    core, x_at, z_at, place = lax.rem(me, 2), lax.rem(me // 2, 2), me // slots, lax.rem(me, slots)
     peer = 1 - seg
     other = me + 1 - 2 * core
     slab_rows = side // 2
@@ -187,13 +190,14 @@
     for k in range(1, line // 2):
         part = lax.rem(z_half + k, line // 2)
         far += [2 * part, 2 * part + 1]
-    after, before = lax.rem(me + 1, frames), lax.rem(me + frames - 1, frames)
+    across = (x_peer, x_peer + 1 - 2 * core)
 
     barrier = pltpu.get_barrier_semaphore()
-    pl.semaphore_signal(barrier, inc=1, device_id=(peer, me), device_id_type=MESH)
-    near = [other, x_peer, after, before] + [frame_of(x_at, z) for z in far + [z_pair]]
+    near = [(seg, other)] + [(seg, f) for f in across]
+    near += [(seg, frame_of(x_at, z)) for z in far + [z_pair]]
+    near += [(peer, f) for f in (me, other) + across]
     for target in near:
-        pl.semaphore_signal(barrier, inc=1, device_id=(seg, target), device_id_type=MESH)
+        pl.semaphore_signal(barrier, inc=1, device_id=target, device_id_type=MESH)
 
     def columns(which):
         return pl.ds(pl.multiple_of(which * half, half), half)
@@ -305,144 +309,210 @@
         for dx in range(3):
             x[dx, clip, 1 : side + 1, :, where] = shifted[dx].reshape(side, side, width_of)
 
-    def row_sum(x, clip, dy, base):
-        total = None
-        for dx in range(3):
-            view = x[dx, clip, dy : dy + side].reshape(cells, lanes)
-            term = jnp.dot(view, w_ref[base + dx], preferred_element_type=jnp.float32)
-            total = term if total is None else total + term
+    def row_sum(x, clip, rows, base, total=None):
+        for dy in rows:
+            for dx in range(3):
+                view = x[dx, clip, dy : dy + side].reshape(cells, lanes)
+                term = jnp.dot(
+                    view, w_ref[base + width * dy + dx], preferred_element_type=jnp.float32
+                )
+                total = term if total is None else total + term
         return total
 
     def silu(u):
         return u / (1.0 + jnp.exp(-u))
 
-    def a_copy(s, clip):
+    def arrival(j):
+        return jnp.where(j == 0, 0, jnp.where(j == 1, slots - 1, j - 1))
+
+    def departure(j):
+        there = lax.rem(place + slots // 2 * (1 - j // 2), slots)
+        return jnp.where(lax.rem(j, 2) == 0, there + 1 - 2 * lax.rem(there, 2), there)
+
+    def noisy_local():
+        return pltpu.make_async_copy(noisy_ref.at[place, 0], n_ref.at[place], n_sem.at[0])
+
+    def send_noisy(unused):
+        remote(
+            noisy_ref.at[lax.rem(other, slots), 0],
+            n_ref.at[place],
+            n_sem.at[4],
+            n_sem.at[1],
+            (seg, other),
+        ).start()
+        for target in across:
+            remote(
+                noisy_ref.at[lax.rem(target, slots), 0, :, :, columns(seg)],
+                n_ref.at[place, :, :, columns(seg)],
+                n_sem.at[4],
+                n_sem.at[2],
+                (seg, target),
+            ).start()
+
+    def relay_noisy(unused):
+        take(n_ref.at[0], n_sem.at[2])
+        for target in across:
+            ref = n_ref.at[lax.rem(target, slots), :, :, columns(seg)]
+            remote(ref, ref, n_sem.at[4], n_sem.at[3], (peer, me)).start()
+
+    def take_noisy(unused):
+        for i in (0, 1, 3):
+            take(n_ref.at[0], n_sem.at[i])
+
+    def build_noisy(j):
+        slot = arrival(j)
+        build(xe, slot, n_ref[slot].reshape(cells, lanes), slice(None))
+
+    def a_copy(s, slot):
         return remote(
-            a_send.at[s, clip], a_recv.at[s, clip], a_sem.at[2, 0], a_sem.at[s, clip], (peer, me)
-        )
-
-    def e_copy(clip):
-        return remote(e_mine.at[clip], e_recv.at[clip], e_sem.at[1, 0], e_sem.at[0, clip], (peer, me))
-
-    def t_copy(s, way, clip):
-        target = after if way == 0 else before
+            a_send.at[s, slot], a_recv.at[s, slot], a_sem.at[2, 0], a_sem.at[s, slot], (peer, me)
+        )
+
+    def e_copy(slot):
+        return remote(e_mine.at[slot], e_recv.at[slot], e_sem.at[1, 0], e_sem.at[0, slot], (peer, me))
+
+    sends_on = (z_at < line - 1, z_at > 0)
+    takes_on = (z_at > 0, z_at < line - 1)
+
+    def t_copy(s, way):
+        target = me + slots if way == 0 else me - slots
         return remote(
-            t_send.at[way, s, clip],
-            t_recv.at[way, s, clip],
-            t_sem.at[way, 2, 0],
-            t_sem.at[way, s, clip],
-            (seg, target),
-        )
-
-    def o_copy(clip):
+            t_send.at[way, s],
+            t_recv.at[way, s],
+            t_sem.at[way, 2],
+            t_sem.at[way, s],
+            (seg, lax.rem(target + frames, frames)),
+        )
+
+    def o_copy(slot, rows):
         return remote(
-            o_full.at[clip, pl.ds(peer * slab_rows, slab_rows)],
-            out_ref.at[clip, 0, :, :, columns(seg)],
-            o_sem.at[1, 0],
-            o_sem.at[0, clip],
-            (peer, me),
-        )
-
-    def first_row(s, dy):
-        def work(clip):
-            term = row_sum(xe, clip, dy, s * taps + dy * width)
-            acc_ref[clip] = term if dy == 0 else acc_ref[clip] + term
+            o_full.at[2 * slot + rows],
+            out_ref.at[place, 0, :, :, columns(seg)],
+            o_sem.at[1],
+            o_sem.at[0],
+            (rows, z_at * slots + slot),
+        )
+
+    def first_rows(s):
+        def work(j):
+            slot = arrival(j)
+            total = row_sum(xe, slot, range(rows_per_conv), s * taps)
+            a_send[s, slot] = silu(total).astype(jnp.bfloat16)
+            a_copy(s, slot).start()
 
         return work
 
-    def send_active(s):
-        def work(clip):
-            a_send[s, clip] = silu(acc_ref[clip]).astype(jnp.bfloat16)
-            a_copy(s, clip).start()
+    def take_active(s):
+        def work(j):
+            slot = arrival(j)
+            a_copy(s, slot).wait_recv()
+            build(xa, slot + 1, a_send[s, slot], columns(seg))
+            build(xa, slot + 1, a_recv[s, slot], columns(peer))
 
         return work
 
-    def take_active(s):
-        def work(clip):
-            a_copy(s, clip).wait_recv()
-            build(xa, clip, a_send[s, clip], columns(seg))
-            build(xa, clip, a_recv[s, clip], columns(peer))
+    def mixed(s, slot, k):
+        view = xa[1, slot + k, 1 : side + 1].reshape(cells, lanes)
+        return jnp.dot(
+            view, w_ref[s * taps + rows_per_conv * width + k], preferred_element_type=jnp.float32
+        )
+
+    def terms(s):
+        def work(j):
+            for way, slot in ((1, 0), (0, slots - 1)):
+
+                @pl.when((j == 1 - way) & sends_on[way])
+                def _():
+                    view = xa[1, slot + 1, 1 : side + 1].reshape(cells, lanes)
+                    base = s * taps + rows_per_conv * width
+                    t_send[way, s] = jnp.dot(
+                        view, w_ref[base + 2 * way], preferred_element_type=jnp.float32
+                    ).astype(jnp.bfloat16)
+                    t_copy(s, way).start()
 
         return work
 
-    sends_on = (me < frames - 1, me > 0)
-    takes_on = (me > 0, me < frames - 1)
-
-    def terms(s):
-        def work(clip):
-            base = s * taps + rows_per_conv * width
-            view = xa[1, clip, 1 : side + 1].reshape(cells, lanes)
-
-            def mixed(k):
-                return jnp.dot(view, w_ref[base + k], preferred_element_type=jnp.float32)
-
-            for way, k in ((0, 0), (1, 2)):
-                t_send[way, s, clip] = mixed(k).astype(jnp.bfloat16)
-
-                @pl.when(sends_on[way])
-                def _():
-                    t_copy(s, way, clip).start()
-
-            acc_ref[clip] = mixed(1)
+    def second_sum(s, slot, rows, with_time, total=None):
+        base = s * taps + (rows_per_conv + 1) * width
+        total = row_sum(xa, slot + 1, rows, base, total)
+        if with_time:
+            for k in range(width):
+                total = total + mixed(s, slot, k)
+        return total
+
+    def early_rows(s, rows, with_time):
+        def work(j):
+            slot = arrival(j)
+            acc_ref[slot] = second_sum(s, slot, rows, with_time)
 
         return work
 
-    def second_row(s, dy):
-        def work(clip):
-            base = s * taps + (rows_per_conv + 1 + dy) * width
-            acc_ref[clip] = acc_ref[clip] + row_sum(xa, clip, dy, base)
+    def finished(s, slot):
+        for way, edge_slot in ((0, 0), (1, slots - 1)):
+
+            @pl.when(takes_on[way] & (slot == edge_slot))
+            def _():
+                t_copy(s, way).wait_recv()
+                acc_ref[slot] = acc_ref[slot] + t_recv[way, s].astype(jnp.float32)
+
+        return silu(acc_ref[slot])
+
+    def end_first(j):
+        slot = arrival(j)
+        acc_ref[slot] = second_sum(0, slot, range(rows_per_conv), True)
+        mine = n_ref[slot, :, :, columns(seg)].reshape(cells, half).astype(jnp.float32)
+        out = (mine + finished(0, slot)).astype(jnp.bfloat16)
+        e_mine[slot] = ((out.astype(jnp.float32) + mine) * skip_scale).astype(jnp.bfloat16)
+        e_copy(slot).start()
+
+    def take_entering(j):
+        slot = arrival(j)
+        e_copy(slot).wait_recv()
+        build(xe, slot, e_mine[slot], columns(seg))
+        build(xe, slot, e_recv[slot], columns(peer))
+
+    def end_second(rows, with_time):
+        def work(j):
+            slot = departure(j)
+            acc_ref[slot] = second_sum(1, slot, rows, with_time, acc_ref[slot])
+            out = (e_mine[slot].astype(jnp.float32) + finished(1, slot)).astype(jnp.bfloat16)
+            full = out.reshape(2, slab_rows, side, half)
+            for rows_at in range(2):
+                o_full[2 * slot + rows_at] = full[rows_at]
+            o_copy(slot, peer).start()
+
+            @pl.when(slot != place)
+            def _():
+                o_copy(slot, seg).start()
+
+            @pl.when(slot == place)
+            def _():
+                out_ref[place, 0, :, :, columns(seg)] = o_full[2 * slot + seg]
 
         return work
-
-    def finished(s, clip):
-        for way in range(2):
-
-            @pl.when(takes_on[way])
-            def _():
-                t_copy(s, way, clip).wait_recv()
-                acc_ref[clip] = acc_ref[clip] + t_recv[way, s, clip].astype(jnp.float32)
-
-        return silu(acc_ref[clip])
-
-    def end_first(clip):
-        mine = noisy_ref[clip, 0, :, :, columns(seg)].reshape(cells, half).astype(jnp.float32)
-        out = (mine + finished(0, clip)).astype(jnp.bfloat16)
-        e_mine[clip] = ((out.astype(jnp.float32) + mine) * skip_scale).astype(jnp.bfloat16)
-        e_copy(clip).start()
-
-    def take_entering(clip):
-        e_copy(clip).wait_recv()
-        build(xe, clip, e_mine[clip], columns(seg))
-        build(xe, clip, e_recv[clip], columns(peer))
-
-    def end_second(clip):
-        out = (e_mine[clip].astype(jnp.float32) + finished(1, clip)).astype(jnp.bfloat16)
-        o_full[clip] = out.reshape(side, side, half)
-        o_copy(clip).start()
-        out_ref[clip, 0, :, :, columns(seg)] = o_full[clip, pl.ds(seg * slab_rows, slab_rows)]
 
     for j in range(per_section):
         local_copy(j).start()
 
+    noisy_local().start()
     edge = jnp.zeros((side, lanes), jnp.bfloat16)
     for x in (xe, xa):
         for dx in range(3):
 
-            @pl.loop(0, clips)
-            def _(clip):
-                x[dx, clip, 0] = edge
-                x[dx, clip, side + 1] = edge
-
-    @pl.loop(0, clips)
-    def _(clip):
-        build(xe, clip, noisy_ref[clip, 0].reshape(cells, lanes), slice(None))
-
-    pl.semaphore_wait(barrier, len(near) + 1)
+            @pl.loop(0, x.shape[1])
+            def _(slot):
+                x[dx, slot, 0] = edge
+                x[dx, slot, side + 1] = edge
+
+    for slot in (0, slots + 1):
+        xa[1, slot, 1 : side + 1] = jnp.zeros((side, side, lanes), jnp.bfloat16)
+
+    pl.semaphore_wait(barrier, len(near))
 
     for j in range(per_section):
         y_copy(j).start()
 
-    beat = clips
+    beat = slots
     rounds = (
         (0, round_own),
         (3, round_cross),
@@ -454,25 +524,24 @@
     def ready(g):
         return beat * g + rounds[-1][0]
 
-    steps = (
-        ((0, 1, ((0, 1), (0, 1), (0, 1))), (25, 3), (((27, 3), (31, 2), (36, 1)), (38, 1))),
-        ((43, 3, ((43, 3), (44, 3), (47, 2))), (52, 3), (((56, 2), (60, 1), (63, 1)), (64, 1))),
+    every = tuple(range(rows_per_conv))
+    plan = (
+        (1, 1, 1, send_noisy),
+        (9, 1, 1, relay_noisy),
+        (14, 1, 1, take_noisy),
+        (14, 1, slots, build_noisy),
+        (ready(2), 1, slots, first_rows(0)),
+        (25, 3, slots, take_active(0)),
+        (25, 3, 2, terms(0)),
+        (ready(6), 1, slots, end_first),
+        (41, 3, slots, take_entering),
+        (ready(9), 1, slots, first_rows(1)),
+        (52, 3, slots, take_active(1)),
+        (52, 3, 2, terms(1)),
+        (ready(12), 1, slots, early_rows(1, every[:-1], False)),
+        (ready(13), 1, slots, end_second(every[-1:], True)),
     )
-    plan = []
-    for s in range(2):
-        first, mixed_at, second = steps[s]
-        base = per_section * s
-        if s == 1:
-            plan.append((first[0], first[1], take_entering))
-        for dy, (offset, stride) in enumerate(first[2]):
-            plan.append((max(offset, ready(base + dy)), stride, first_row(s, dy)))
-        plan.append((plan[-1][0], plan[-1][1], send_active(s)))
-        plan.append((mixed_at[0], mixed_at[1], take_active(s)))
-        plan.append((max(mixed_at[0], ready(base + 3)), mixed_at[1], terms(s)))
-        for dy, (offset, stride) in enumerate(second[0]):
-            plan.append((max(offset, ready(base + 4 + dy)), stride, second_row(s, dy)))
-        plan.append((second[1][0], second[1][1], end_first if s == 0 else end_second))
-    last = max(offset + stride * (clips - 1) + 1 for offset, stride, _ in plan)
+    last = max(offset + stride * (count - 1) + 1 for offset, stride, count, _ in plan)
 
     @pl.loop(0, last)
     def _(step):
@@ -483,25 +552,23 @@
             def _():
                 work(at // beat)
 
-        for offset, stride, work in plan:
+        for offset, stride, count, work in plan:
             at = step - offset
 
-            @pl.when((at >= 0) & (lax.rem(at, stride) == 0) & (at < stride * clips))
+            @pl.when((at >= 0) & (lax.rem(at, stride) == 0) & (at < stride * count))
             def _():
                 work(at // stride)
 
-    @pl.loop(0, clips)
-    def _(clip):
-        o_copy(clip).wait_recv()
-
-    take(o_full.at[:, pl.ds(0, slab_rows)], o_sem.at[1, 0])
+    for i in range(2):
+        take(o_full.at[pl.ds(0, 2 * slots - 1)], o_sem.at[i])
+    take(n_ref.at[pl.ds(0, 3)], n_sem.at[4])
     take(e_mine, e_sem.at[1, 0])
     take(a_send, a_sem.at[2, 0])
     for way in range(2):
 
         @pl.when(sends_on[way])
         def _():
-            take(t_send.at[way], t_sem.at[way, 2, 0])
+            take(t_send.at[way], t_sem.at[way, 2])
 
     take(w_ref.at[pl.ds(0, taps), pl.ds(0, depth)], y_sem.at[per_section])
     for link, count in enumerate((line - 1, line, 2 * line)):
@@ -514,7 +581,7 @@
     clips, frame_local, side, _, lanes = noisy_clips.shape
     half = lanes // 2
     cells = side * side
-    if sections != 2 or half % 128 or frames % 8 or frames < 16 or frame_local != 1 or side % 16:
+    if sections != 2 or half % 128 or frames % 8 or frames < 16 or clips != 4 or frame_local != 1 or side % 16:
         return pipelined(noisy_clips, conv_first, conv_second, temporal)
     taps = conv_first.shape[1] + temporal.shape[1] + conv_second.shape[1]
     per_section = taps // temporal.shape[1]
@@ -524,28 +591,30 @@
     return pl.pallas_call(
         functools.partial(fused_kernel, frames),
         out_shape=jax.ShapeDtypeStruct((clips, 1, side // 2, side, lanes), kind),
-        in_specs=[vmem] + [pl.BlockSpec(memory_space=pl.ANY)] * 3,
+        in_specs=[pl.BlockSpec(memory_space=pl.ANY)] * 4,
         out_specs=vmem,
         scratch_shapes=[
             pltpu.VMEM((2 * taps, lanes, half), kind),
+            pltpu.VMEM((clips, side, side, lanes), kind),
             pltpu.VMEM((3, clips, side + 2, side, lanes), kind),
-            pltpu.VMEM((3, clips, side + 2, side, lanes), kind),
+            pltpu.VMEM((3, clips + 2, side + 2, side, lanes), kind),
             pltpu.VMEM((2, clips, cells, half), kind),
             pltpu.VMEM((2, clips, cells, half), kind),
-            pltpu.VMEM((2, 2, clips, cells, half), kind),
-            pltpu.VMEM((2, 2, clips, cells, half), kind),
+            pltpu.VMEM((2, 2, cells, half), kind),
+            pltpu.VMEM((2, 2, cells, half), kind),
             pltpu.VMEM((clips, cells, half), kind),
             pltpu.VMEM((clips, cells, half), kind),
             pltpu.VMEM((clips, cells, half), jnp.float32),
-            pltpu.VMEM((clips, side, side, half), kind),
+            pltpu.VMEM((2 * clips, side // 2, side, half), kind),
             dma((per_section,)),
+            dma((5,)),
             dma((per_section + 1,)),
             dma((4, 2 * per_section)),
             dma((3,)),
             dma((3, clips)),
-            dma((2, 3, clips)),
+            dma((2, 3)),
             dma((2, clips)),
-            dma((2, clips)),
+            dma((2,)),
         ],
         compiler_params=pltpu.CompilerParams(
             collective_id=0, has_side_effects=True, vmem_limit_bytes=58 * 1024 * 1024

time: 103 us -> 92.5 us (0.90)
  the two profiles are of different devices: /device:TPU:28 before, /device:TPU:0 now
where the time goes in v2:
time: 92.5 us; the launch traced here: 92.3 us
  Pallas kernels  90.5 us (98%)
  local copies, waits for them, and re-layouts  1.87 us (2%)
    pallas_call x1, Pallas kernels, on_device(): pl.pallas_call(functools.partial(fused_kernel, frames), out_shape=jax.Sha...  90.5 us
    unnamed x1, local copies, waits for them, and re-layouts  1.87 us

profile of v2, /device:TPU:0, one launch (start us, length us, event | category | flops | bytes accessed | tf_op | source)
XLA Modules:
  0.0 92.3 jit_solution(6662322307232720446)
XLA Ops:
  0.0 90.5 %shard_map.46 = bf16[4,1,8,16,512]{4,3,2,1,0:T(8,128)(2,1)} custom-call(bf16[4,1,16,16,512]{4,3,2,1,0:T(8,128)(2,1)} %noisy_ref.1, bf16[1,9,32,512]{3,2,1,0:T(8,128)(2,1)} %first_ref.1, bf16[1,9,32,512]{3,2,1,0:T(8,128)(2,1)} %second_ref.1, bf16[1,3,32,512]{3,2,1,0:T(8,128)(2,1)} %time_ref.1), custom_call_target="tpu_custom_call" | custom-call | tf_op jit(solution)/shard_map/pallas_call | solution.py:591
  90.5 1.9 %copy.6 = bf16[4,1,8,16,512]{4,3,2,1,0:T(8,128)(2,1)} copy(bf16[4,1,8,16,512]{4,3,2,1,0:T(8,128)(2,1)} %shard_map.46) | data formatting | bytes 1048576

commit v3 on v2

--- a/solution.py
+++ b/solution.py
@@ -186,15 +186,14 @@
     x_peer = frame_of(1 - x_at, z_at)
     z_pair = z_at + 1 - 2 * lax.rem(z_at, 2)
     z_half = z_at // 2
-    far = []
-    for k in range(1, line // 2):
-        part = lax.rem(z_half + k, line // 2)
-        far += [2 * part, 2 * part + 1]
+    inner = lax.rem(z_at, 2) != z_half
+    z_near, z_end = 2 - z_half, 3 - 3 * z_half
+    far = (z_near, z_end)
     across = (x_peer, x_peer + 1 - 2 * core)
 
     barrier = pltpu.get_barrier_semaphore()
     near = [(seg, other)] + [(seg, f) for f in across]
-    near += [(seg, frame_of(x_at, z)) for z in far + [z_pair]]
+    near += [(seg, frame_of(x_at, z)) for z in far + (z_pair,)]
     near += [(peer, f) for f in (me, other) + across]
     for target in near:
         pl.semaphore_signal(barrier, inc=1, device_id=target, device_id_type=MESH)
@@ -204,6 +203,8 @@
 
     def rows_of(owner):
         return pl.ds(pl.multiple_of(owner * depth, depth), depth)
+
+    crossing = [g % 2 < 1 for g in range(groups)]
 
     def part(j):
         if j < rows_per_conv:
@@ -249,7 +250,7 @@
     def some(g, count):
         return w_ref.at[pl.ds(g * width, width), pl.ds(0, count * depth)]
 
-    own, crossed, lined, rest = 0, 1, 2, 3
+    own, crossed, lined, paired, rest = range(5)
 
     def give(g, owner, kind, link, target):
         ref = slab(g, owner)
@@ -270,28 +271,51 @@
             take(slab(g, me), y_sem.at[j])
 
         give(g, me, crossed, 0, x_peer)
-        for z in far:
-            give(g, me, lined, 1, frame_of(x_at, z))
-        give(g, me, rest, 1, frame_of(x_at, z_pair))
+        give(g, me, lined, 1, frame_of(x_at, z_near))
+
+        @pl.when(inner)
+        def _():
+            give(g, me, lined, 1, frame_of(x_at, z_end))
+
+        give(g, me, paired, 1, frame_of(x_at, z_pair))
         give_core(g, me)
+
+    def crosses(g):
+        return lax.rem(g, 2) < 1
 
     def round_cross(g):
         take(some(g, 1), got_sem.at[crossed, g])
-        give(g, x_peer, rest, 1, frame_of(x_at, z_pair))
+
+        @pl.when(crosses(g))
+        def _():
+            give(g, x_peer, rest, 1, frame_of(x_at, z_pair))
+
         give_core(g, x_peer)
 
     def round_line(g):
-        take(some(g, len(far)), got_sem.at[lined, g])
+        take(some(g, 2), got_sem.at[lined, g])
+
+        @pl.when(inner)
+        def _():
+            give(g, frame_of(x_at, z_end), lined, 1, frame_of(x_at, z_pair))
+
         for z in far:
             give(g, frame_of(x_at, z), rest, 0, x_peer)
         for z in far:
             give_core(g, frame_of(x_at, z))
 
+    def round_pair(g):
+        take(some(g, 1), got_sem.at[paired, g])
+
+        @pl.when(jnp.logical_not(crosses(g)))
+        def _():
+            give(g, frame_of(x_at, z_pair), rest, 0, x_peer)
+
+        give_core(g, frame_of(x_at, z_pair))
+
     def round_rest(g):
-        take(some(g, len(far) + 2), got_sem.at[rest, g])
-        give_core(g, frame_of(x_at, z_pair))
-        give_core(g, frame_of(1 - x_at, z_pair))
-        for z in far:
+        take(some(g, 3), got_sem.at[rest, g])
+        for z in far + (z_pair,):
             give_core(g, frame_of(1 - x_at, z))
 
     def round_done(g):
@@ -516,9 +540,10 @@
     rounds = (
         (0, round_own),
         (3, round_cross),
-        (5, round_line),
-        (9, round_rest),
-        (11, round_done),
+        (jnp.where(inner, 5, 9), round_line),
+        (6, round_pair),
+        (13, round_rest),
+        (16, round_done),
     )
 
     def ready(g):
@@ -531,15 +556,15 @@
         (14, 1, 1, take_noisy),
         (14, 1, slots, build_noisy),
         (ready(2), 1, slots, first_rows(0)),
-        (25, 3, slots, take_active(0)),
-        (25, 3, 2, terms(0)),
-        (ready(6), 1, slots, end_first),
-        (41, 3, slots, take_entering),
-        (ready(9), 1, slots, first_rows(1)),
-        (52, 3, slots, take_active(1)),
-        (52, 3, 2, terms(1)),
-        (ready(12), 1, slots, early_rows(1, every[:-1], False)),
-        (ready(13), 1, slots, end_second(every[-1:], True)),
+        (ready(2) + 6, 3, slots, take_active(0)),
+        (ready(2) + 6, 3, 2, terms(0)),
+        (ready(6) + 0, 1, slots, end_first),
+        (ready(6) + 5, 3, slots, take_entering),
+        (ready(9) + 0, 1, slots, first_rows(1)),
+        (ready(9) + 5, 3, slots, take_active(1)),
+        (ready(9) + 5, 3, 2, terms(1)),
+        (ready(12) + 0, 1, slots, early_rows(1, every[:-1], False)),
+        (ready(13) + 0, 1, slots, end_second(every[-1:], True)),
     )
     last = max(offset + stride * (count - 1) + 1 for offset, stride, count, _ in plan)
 
@@ -571,8 +596,21 @@
             take(t_send.at[way], t_sem.at[way, 2])
 
     take(w_ref.at[pl.ds(0, taps), pl.ds(0, depth)], y_sem.at[per_section])
-    for link, count in enumerate((line - 1, line, 2 * line)):
-        take(w_ref.at[:, pl.ds(0, count * depth)], sent_sem.at[link])
+    def sent(link, count):
+        high = max(k for k in range(1, groups + 1) if count % k == 0)
+        take(w_ref.at[pl.ds(0, high * width), pl.ds(0, count // high * depth)], sent_sem.at[link])
+
+    crossings = sum(crossing)
+    sent(0, 3 * groups + groups - crossings)
+    sent(2, 2 * line * groups)
+
+    @pl.when(inner)
+    def _():
+        sent(1, 4 * groups + crossings)
+
+    @pl.when(jnp.logical_not(inner))
+    def _():
+        sent(1, 2 * groups + crossings)
 
 
 def on_device(noisy_clips, conv_first, conv_second, temporal):
@@ -581,7 +619,7 @@
     clips, frame_local, side, _, lanes = noisy_clips.shape
     half = lanes // 2
     cells = side * side
-    if sections != 2 or half % 128 or frames % 8 or frames < 16 or clips != 4 or frame_local != 1 or side % 16:
+    if sections != 2 or half % 128 or frames != 16 or clips != 4 or frame_local != 1 or side % 16:
         return pipelined(noisy_clips, conv_first, conv_second, temporal)
     taps = conv_first.shape[1] + temporal.shape[1] + conv_second.shape[1]
     per_section = taps // temporal.shape[1]
@@ -609,7 +647,7 @@
             dma((per_section,)),
             dma((5,)),
             dma((per_section + 1,)),
-            dma((4, 2 * per_section)),
+            dma((5, 2 * per_section)),
             dma((3,)),
             dma((3, clips)),
             dma((2, 3)),

time: 92.5 us -> 92.7 us (level)
  no operation moved by 1% of the time
where the time goes in v3:
time: 92.7 us; the launch traced here: 92.5 us
  Pallas kernels  90.7 us (98%)
  local copies, waits for them, and re-layouts  1.87 us (2%)
    pallas_call x1, Pallas kernels, on_device(): pl.pallas_call(functools.partial(fused_kernel, frames), out_shape=jax.Sha...  90.7 us
    unnamed x1, local copies, waits for them, and re-layouts  1.87 us

profile of v3, /device:TPU:0, one launch (start us, length us, event | category | flops | bytes accessed | tf_op | source)
XLA Modules:
  0.0 92.5 jit_solution(592940341329008102)
XLA Ops:
  0.0 90.7 %shard_map.46 = bf16[4,1,8,16,512]{4,3,2,1,0:T(8,128)(2,1)} custom-call(bf16[4,1,16,16,512]{4,3,2,1,0:T(8,128)(2,1)} %noisy_ref.1, bf16[1,9,32,512]{3,2,1,0:T(8,128)(2,1)} %first_ref.1, bf16[1,9,32,512]{3,2,1,0:T(8,128)(2,1)} %second_ref.1, bf16[1,3,32,512]{3,2,1,0:T(8,128)(2,1)} %time_ref.1), custom_call_target="tpu_custom_call" | custom-call | tf_op jit(solution)/shard_map/pallas_call | solution.py:629
  90.7 1.9 %copy.6 = bf16[4,1,8,16,512]{4,3,2,1,0:T(8,128)(2,1)} copy(bf16[4,1,8,16,512]{4,3,2,1,0:T(8,128)(2,1)} %shard_map.46) | data formatting | bytes 1048576

commit v4 on v3

--- a/solution.py
+++ b/solution.py
@@ -131,6 +131,43 @@
     delivered = broadcast(final_carry[2], "segment", sections - 1)
     slab_rows = side_len // sections
     return lax.dynamic_slice_in_dim(delivered, segment_id * slab_rows, slab_rows, 2)
+
+
+CODE, PACK, EVENTS = 16, 3, 127
+ORDERS = (
+    (
+        131328, 3149920, 1192209, 6357810, 1246240, 7341363, 4203041, 3428372,
+        3478790, 475446, 4346147, 8486948, 9458198, 3610513, 4428418, 2462595,
+        4458579, 5514761, 11575306, 1590539, 11641173, 3680025, 1745478, 1791545,
+        3842856, 12666816, 3916375, 2736968, 839768, 13712397, 1845833, 2856025,
+        13800733, 4861078, 4954067, 11838554, 4996443, 11885733, 14757344, 5104294,
+        6153127, 15921648, 243,
+    ),
+    (
+        131328, 3149920, 1192209, 6357810, 1246259, 7341344, 1319457, 406592,
+        1409408, 8540213, 4273795, 5317383, 2361410, 9458198, 9574289, 4428581,
+        596128, 5480759, 3715504, 10638404, 1656102, 697173, 735558, 12589654,
+        2670887, 3850779, 3877315, 839751, 5720077, 5782737, 2806345, 1872985,
+        2856253, 4888093, 2922451, 11838554, 10825035, 5004213, 14703782, 14868813,
+        14919517, 15921648, 243,
+    ),
+    (
+        131328, 1118304, 3146528, 2167393, 2233137, 278578, 348272, 3351302,
+        4346177, 1324068, 464210, 3482902, 8491136, 8556867, 4470310, 1544787,
+        11575380, 3614595, 4524179, 5616033, 4589880, 2643618, 673593, 1622691,
+        12801817, 3869498, 793129, 13769544, 12593752, 2867529, 9853212, 9818442,
+        2906684, 9915347, 9722832, 894525, 14834764, 14888359, 11838493, 10833376,
+        14769589, 15921648, 243,
+    ),
+    (
+        131328, 1118304, 3153923, 2167393, 2233137, 278578, 348272, 3351302,
+        8409409, 8536705, 1324068, 9458307, 2461973, 9573941, 476051, 5449224,
+        4497462, 5507504, 3614625, 1525169, 1614421, 4601896, 1641123, 12829270,
+        4667689, 13784843, 12651592, 12605466, 13842986, 1772873, 2856537, 9903163,
+        9752650, 2906653, 9818428, 4009291, 5023323, 10871388, 5104053, 6153127,
+        14726308, 15921648, 243,
+    ),
+)
 
 
 def fused_kernel(
@@ -205,6 +242,7 @@
         return pl.ds(pl.multiple_of(owner * depth, depth), depth)
 
     crossing = [g % 2 < 1 for g in range(groups)]
+    every = tuple(range(rows_per_conv))
 
     def part(j):
         if j < rows_per_conv:
@@ -347,7 +385,8 @@
         return u / (1.0 + jnp.exp(-u))
 
     def arrival(j):
-        return jnp.where(j == 0, 0, jnp.where(j == 1, slots - 1, j - 1))
+        slot = jnp.where(j == 0, 0, jnp.where(j == 1, slots - 1, j - 1))
+        return jnp.where(z_half == 0, slot, slots - 1 - slot)
 
     def departure(j):
         there = lax.rem(place + slots // 2 * (1 - j // 2), slots)
@@ -356,22 +395,25 @@
     def noisy_local():
         return pltpu.make_async_copy(noisy_ref.at[place, 0], n_ref.at[place], n_sem.at[0])
 
-    def send_noisy(unused):
+    def send_noisy(part_at):
+        @pl.when(part_at == 0)
+        def _():
+            remote(
+                noisy_ref.at[lax.rem(other, slots), 0],
+                n_ref.at[place],
+                n_sem.at[4],
+                n_sem.at[1],
+                (seg, other),
+            ).start()
+
+        target = jnp.where(part_at == 0, across[0], across[1])
         remote(
-            noisy_ref.at[lax.rem(other, slots), 0],
-            n_ref.at[place],
+            noisy_ref.at[lax.rem(target, slots), 0, :, :, columns(seg)],
+            n_ref.at[place, :, :, columns(seg)],
             n_sem.at[4],
-            n_sem.at[1],
-            (seg, other),
+            n_sem.at[2],
+            (seg, target),
         ).start()
-        for target in across:
-            remote(
-                noisy_ref.at[lax.rem(target, slots), 0, :, :, columns(seg)],
-                n_ref.at[place, :, :, columns(seg)],
-                n_sem.at[4],
-                n_sem.at[2],
-                (seg, target),
-            ).start()
 
     def relay_noisy(unused):
         take(n_ref.at[0], n_sem.at[2])
@@ -379,11 +421,12 @@
             ref = n_ref.at[lax.rem(target, slots), :, :, columns(seg)]
             remote(ref, ref, n_sem.at[4], n_sem.at[3], (peer, me)).start()
 
-    def take_noisy(unused):
-        for i in (0, 1, 3):
-            take(n_ref.at[0], n_sem.at[i])
-
     def build_noisy(j):
+        @pl.when(j == 0)
+        def _():
+            for i in (0, 1, 3):
+                take(n_ref.at[0], n_sem.at[i])
+
         slot = arrival(j)
         build(xe, slot, n_ref[slot].reshape(cells, lanes), slice(None))
 
@@ -417,23 +460,17 @@
             (rows, z_at * slots + slot),
         )
 
-    def first_rows(s):
-        def work(j):
-            slot = arrival(j)
-            total = row_sum(xe, slot, range(rows_per_conv), s * taps)
-            a_send[s, slot] = silu(total).astype(jnp.bfloat16)
-            a_copy(s, slot).start()
-
-        return work
-
-    def take_active(s):
-        def work(j):
-            slot = arrival(j)
-            a_copy(s, slot).wait_recv()
-            build(xa, slot + 1, a_send[s, slot], columns(seg))
-            build(xa, slot + 1, a_recv[s, slot], columns(peer))
-
-        return work
+    def first_rows(turn):
+        s, slot = lax.div(turn, slots), arrival(lax.rem(turn, slots))
+        total = row_sum(xe, slot, every, s * taps)
+        a_send[s, slot] = silu(total).astype(jnp.bfloat16)
+        a_copy(s, slot).start()
+
+    def take_active(turn):
+        s, slot = lax.div(turn, slots), arrival(lax.rem(turn, slots))
+        a_copy(s, slot).wait_recv()
+        build(xa, slot + 1, a_send[s, slot], columns(seg))
+        build(xa, slot + 1, a_recv[s, slot], columns(peer))
 
     def mixed(s, slot, k):
         view = xa[1, slot + k, 1 : side + 1].reshape(cells, lanes)
@@ -441,20 +478,18 @@
             view, w_ref[s * taps + rows_per_conv * width + k], preferred_element_type=jnp.float32
         )
 
-    def terms(s):
-        def work(j):
-            for way, slot in ((1, 0), (0, slots - 1)):
-
-                @pl.when((j == 1 - way) & sends_on[way])
-                def _():
-                    view = xa[1, slot + 1, 1 : side + 1].reshape(cells, lanes)
-                    base = s * taps + rows_per_conv * width
-                    t_send[way, s] = jnp.dot(
-                        view, w_ref[base + 2 * way], preferred_element_type=jnp.float32
-                    ).astype(jnp.bfloat16)
-                    t_copy(s, way).start()
-
-        return work
+    def terms(turn):
+        s, slot = lax.div(turn, slots), arrival(lax.rem(turn, slots))
+        view = xa[1, slot + 1, 1 : side + 1].reshape(cells, lanes)
+        base = s * taps + rows_per_conv * width
+        for way, edge_slot in ((1, 0), (0, slots - 1)):
+
+            @pl.when((slot == edge_slot) & sends_on[way])
+            def _():
+                t_send[way, s] = jnp.dot(
+                    view, w_ref[base + 2 * way], preferred_element_type=jnp.float32
+                ).astype(jnp.bfloat16)
+                t_copy(s, way).start()
 
     def second_sum(s, slot, rows, with_time, total=None):
         base = s * taps + (rows_per_conv + 1) * width
@@ -464,12 +499,9 @@
                 total = total + mixed(s, slot, k)
         return total
 
-    def early_rows(s, rows, with_time):
-        def work(j):
-            slot = arrival(j)
-            acc_ref[slot] = second_sum(s, slot, rows, with_time)
-
-        return work
+    def early_rows(j):
+        slot = arrival(j)
+        acc_ref[slot] = second_sum(1, slot, every[:-1], False)
 
     def finished(s, slot):
         for way, edge_slot in ((0, 0), (1, slots - 1)):
@@ -483,7 +515,7 @@
 
     def end_first(j):
         slot = arrival(j)
-        acc_ref[slot] = second_sum(0, slot, range(rows_per_conv), True)
+        acc_ref[slot] = second_sum(0, slot, every, True)
         mine = n_ref[slot, :, :, columns(seg)].reshape(cells, half).astype(jnp.float32)
         out = (mine + finished(0, slot)).astype(jnp.bfloat16)
         e_mine[slot] = ((out.astype(jnp.float32) + mine) * skip_scale).astype(jnp.bfloat16)
@@ -495,25 +527,60 @@
         build(xe, slot, e_mine[slot], columns(seg))
         build(xe, slot, e_recv[slot], columns(peer))
 
-    def end_second(rows, with_time):
-        def work(j):
-            slot = departure(j)
-            acc_ref[slot] = second_sum(1, slot, rows, with_time, acc_ref[slot])
-            out = (e_mine[slot].astype(jnp.float32) + finished(1, slot)).astype(jnp.bfloat16)
-            full = out.reshape(2, slab_rows, side, half)
-            for rows_at in range(2):
-                o_full[2 * slot + rows_at] = full[rows_at]
-            o_copy(slot, peer).start()
-
-            @pl.when(slot != place)
-            def _():
-                o_copy(slot, seg).start()
-
-            @pl.when(slot == place)
-            def _():
-                out_ref[place, 0, :, :, columns(seg)] = o_full[2 * slot + seg]
-
-        return work
+    def end_second(j):
+        slot = departure(j)
+        acc_ref[slot] = second_sum(1, slot, every[-1:], True, acc_ref[slot])
+        out = (e_mine[slot].astype(jnp.float32) + finished(1, slot)).astype(jnp.bfloat16)
+        full = out.reshape(2, slab_rows, side, half)
+        for rows_at in range(2):
+            o_full[2 * slot + rows_at] = full[rows_at]
+        o_copy(slot, peer).start()
+
+        @pl.when(slot != place)
+        def _():
+            o_copy(slot, seg).start()
+
+        @pl.when(slot == place)
+        def _():
+            out_ref[place, 0, :, :, columns(seg)] = o_full[2 * slot + seg]
+
+    works = (
+        round_own,
+        round_cross,
+        round_line,
+        round_pair,
+        round_rest,
+        round_done,
+        send_noisy,
+        relay_noisy,
+        build_noisy,
+        first_rows,
+        take_active,
+        terms,
+        end_first,
+        take_entering,
+        early_rows,
+        end_second,
+    )
+
+    words = []
+    for codes in zip(*ORDERS):
+        ends, inners = (jnp.where(seg == 0, codes[n], codes[n + 1]) for n in (0, 2))
+        words.append(jnp.where(inner, inners, ends))
+
+    def run(some_works, kind, turn, low=0):
+        if len(some_works) == 1:
+            some_works[0](turn)
+            return
+        cut = len(some_works) // 2
+
+        @pl.when(kind < low + cut)
+        def _():
+            run(some_works[:cut], kind, turn, low)
+
+        @pl.when(kind >= low + cut)
+        def _():
+            run(some_works[cut:], kind, turn, low + cut)
 
     for j in range(per_section):
         local_copy(j).start()
@@ -536,53 +603,21 @@
     for j in range(per_section):
         y_copy(j).start()
 
-    beat = slots
-    rounds = (
-        (0, round_own),
-        (3, round_cross),
-        (jnp.where(inner, 5, 9), round_line),
-        (6, round_pair),
-        (13, round_rest),
-        (16, round_done),
-    )
-
-    def ready(g):
-        return beat * g + rounds[-1][0]
-
-    every = tuple(range(rows_per_conv))
-    plan = (
-        (1, 1, 1, send_noisy),
-        (9, 1, 1, relay_noisy),
-        (14, 1, 1, take_noisy),
-        (14, 1, slots, build_noisy),
-        (ready(2), 1, slots, first_rows(0)),
-        (ready(2) + 6, 3, slots, take_active(0)),
-        (ready(2) + 6, 3, 2, terms(0)),
-        (ready(6) + 0, 1, slots, end_first),
-        (ready(6) + 5, 3, slots, take_entering),
-        (ready(9) + 0, 1, slots, first_rows(1)),
-        (ready(9) + 5, 3, slots, take_active(1)),
-        (ready(9) + 5, 3, 2, terms(1)),
-        (ready(12) + 0, 1, slots, early_rows(1, every[:-1], False)),
-        (ready(13) + 0, 1, slots, end_second(every[-1:], True)),
-    )
-    last = max(offset + stride * (count - 1) + 1 for offset, stride, count, _ in plan)
-
-    @pl.loop(0, last)
-    def _(step):
-        for lag, work in reversed(rounds):
-            at = step - lag
-
-            @pl.when((at >= 0) & (lax.rem(at, beat) == 0) & (at < beat * groups))
-            def _():
-                work(at // beat)
-
-        for offset, stride, count, work in plan:
-            at = step - offset
-
-            @pl.when((at >= 0) & (lax.rem(at, stride) == 0) & (at < stride * count))
-            def _():
-                work(at // stride)
+    @pl.loop(0, EVENTS)
+    def _(i):
+        at, level = i // PACK, words
+        while len(level) > 1:
+            odd = lax.rem(at, 2) == 1
+            level = [
+                jnp.where(odd, level[n + 1], level[n]) if n + 1 < len(level) else level[n]
+                for n in range(0, len(level), 2)
+            ]
+            at = at // 2
+        code = level[0]
+        for n in range(1, PACK):
+            code = jnp.where(lax.rem(i, PACK) == n, level[0] // (CODE * CODE) ** n, code)
+        code = lax.rem(code, CODE * CODE)
+        run(works, code // CODE, lax.rem(code, CODE))
 
     for i in range(2):
         take(o_full.at[pl.ds(0, 2 * slots - 1)], o_sem.at[i])

time: 92.7 us -> 88.6 us (0.956)
  Pallas kernels: 90.7 us -> 86.6 us
    pallas_call x1, Pallas kernels: 90.7 us -> 86.6 us  [on_device(): pl.pallas_call(functools.partial(fused_kernel, frames), out_shape=jax.Sha...]
where the time goes in v4:
time: 88.6 us; the launch traced here: 88.4 us
  Pallas kernels  86.6 us (98%)
  local copies, waits for them, and re-layouts  1.87 us (2%)
    pallas_call x1, Pallas kernels, on_device(): pl.pallas_call(functools.partial(fused_kernel, frames), out_shape=jax.Sha...  86.6 us
    unnamed x1, local copies, waits for them, and re-layouts  1.87 us

profile of v4, /device:TPU:0, one launch (start us, length us, event | category | flops | bytes accessed | tf_op | source)
XLA Modules:
  0.0 88.4 jit_solution(6185857015716960724)
XLA Ops:
  0.0 86.6 %shard_map.46 = bf16[4,1,8,16,512]{4,3,2,1,0:T(8,128)(2,1)} custom-call(bf16[4,1,16,16,512]{4,3,2,1,0:T(8,128)(2,1)} %noisy_ref.1, bf16[1,9,32,512]{3,2,1,0:T(8,128)(2,1)} %first_ref.1, bf16[1,9,32,512]{3,2,1,0:T(8,128)(2,1)} %second_ref.1, bf16[1,3,32,512]{3,2,1,0:T(8,128)(2,1)} %time_ref.1), custom_call_target="tpu_custom_call" | custom-call | tf_op jit(solution)/shard_map/pallas_call | solution.py:664
  86.6 1.9 %copy.6 = bf16[4,1,8,16,512]{4,3,2,1,0:T(8,128)(2,1)} copy(bf16[4,1,8,16,512]{4,3,2,1,0:T(8,128)(2,1)} %shard_map.46) | data formatting | bytes 1048576

commit v5 on v4

--- a/solution.py
+++ b/solution.py
@@ -136,38 +136,39 @@
 CODE, PACK, EVENTS = 16, 3, 127
 ORDERS = (
     (
-        131328, 3149920, 1192209, 6357810, 1246240, 7341363, 4203041, 3428372,
-        3478790, 475446, 4346147, 8486948, 9458198, 3610513, 4428418, 2462595,
-        4458579, 5514761, 11575306, 1590539, 11641173, 3680025, 1745478, 1791545,
-        3842856, 12666816, 3916375, 2736968, 839768, 13712397, 1845833, 2856025,
-        13800733, 4861078, 4954067, 11838554, 4996443, 11885733, 14757344, 5104294,
-        6153127, 15921648, 243,
+        6291712, 221442, 1126416, 3277873, 332339, 1253488, 406548, 464161,
+        4203061, 544822, 3613462, 8486977, 2392599, 623441, 5380162, 9539640,
+        9577795, 5449363, 723524, 2577433, 4536588, 10507578, 2639536, 10573338,
+        859057, 5750855, 3908124, 10693057, 12729416, 5817130, 2871325, 9722185,
+        9818429, 13773898, 2968470, 13851482, 6048919, 11838541, 10837472, 10936757,
+        11002609, 15983602, 240,
     ),
     (
-        131328, 3149920, 1192209, 6357810, 1246259, 7341344, 1319457, 406592,
-        1409408, 8540213, 4273795, 5317383, 2361410, 9458198, 9574289, 4428581,
-        596128, 5480759, 3715504, 10638404, 1656102, 697173, 735558, 12589654,
-        2670887, 3850779, 3877315, 839751, 5720077, 5782737, 2806345, 1872985,
-        2856253, 4888093, 2922451, 11838554, 10825035, 5004213, 14703782, 14868813,
-        14919517, 15921648, 243,
+        6291712, 221442, 1126416, 3277873, 332339, 1253488, 3409428, 8486945,
+        8618517, 2230069, 3544640, 2295888, 1524023, 2361681, 5380162, 9539640,
+        9577795, 5449363, 11575321, 11641156, 742410, 2573730, 3757324, 3842886,
+        12604954, 4668353, 3981864, 5712323, 13638683, 13715469, 4794968, 1954365,
+        9802841, 9849387, 13851180, 11838615, 10832685, 5004213, 14703782, 14868813,
+        15837021, 15983602, 240,
     ),
     (
-        131328, 1118304, 3146528, 2167393, 2233137, 278578, 348272, 3351302,
-        4346177, 1324068, 464210, 3482902, 8491136, 8556867, 4470310, 1544787,
-        11575380, 3614595, 4524179, 5616033, 4589880, 2643618, 673593, 1622691,
-        12801817, 3869498, 793129, 13769544, 12593752, 2867529, 9853212, 9818442,
-        2906684, 9915347, 9722832, 894525, 14834764, 14888359, 11838493, 10833376,
-        14769589, 15921648, 243,
+        6291712, 221442, 2101520, 1180720, 340257, 3285616, 2295315, 4199475,
+        4280327, 1389604, 2426961, 8405557, 5379713, 4428176, 8533542, 1528722,
+        3642243, 599876, 676888, 4536360, 5615776, 2704907, 11641145, 4656214,
+        2767522, 1726233, 3916451, 4768555, 5770523, 13781308, 5844161, 4898966,
+        3002652, 5936445, 4954067, 9752605, 6048859, 5104294, 14919517, 15971749,
+        11838689, 15786226, 241,
     ),
     (
-        131328, 1118304, 3153923, 2167393, 2233137, 278578, 348272, 3351302,
-        8409409, 8536705, 1324068, 9458307, 2461973, 9573941, 476051, 5449224,
-        4497462, 5507504, 3614625, 1525169, 1614421, 4601896, 1641123, 12829270,
-        4667689, 13784843, 12651592, 12605466, 13842986, 1772873, 2856537, 9903163,
-        9752650, 2906653, 9818428, 4009291, 5023323, 10871388, 5104053, 6153127,
-        14726308, 15921648, 243,
+        6291712, 221442, 2101520, 1180720, 340257, 3285616, 2295315, 8393779,
+        8552768, 5244803, 3417153, 545045, 4338981, 9458198, 2507665, 9671222,
+        10491731, 2570160, 11641156, 5507352, 2662922, 10700088, 4590421, 5639225,
+        4702658, 12632873, 1710423, 866858, 13769544, 2825304, 4838203, 5848108,
+        4888470, 5936593, 1916205, 13650854, 5983380, 11904348, 5104353, 6153127,
+        11838707, 14742257, 240,
     ),
 )
+DIRECT, SHARES = 0, ((1, 3), (2, 5))
 
 
 def fused_kernel(
@@ -241,7 +242,6 @@
     def rows_of(owner):
         return pl.ds(pl.multiple_of(owner * depth, depth), depth)
 
-    crossing = [g % 2 < 1 for g in range(groups)]
     every = tuple(range(rows_per_conv))
 
     def part(j):
@@ -311,20 +311,21 @@
         give(g, me, crossed, 0, x_peer)
         give(g, me, lined, 1, frame_of(x_at, z_near))
 
-        @pl.when(inner)
+        @pl.when(inner | (g < DIRECT))
         def _():
             give(g, me, lined, 1, frame_of(x_at, z_end))
 
         give(g, me, paired, 1, frame_of(x_at, z_pair))
         give_core(g, me)
 
-    def crosses(g):
-        return lax.rem(g, 2) < 1
+    def crosses(g, is_inner):
+        end, mid = (lax.rem(g, share[1]) < share[0] for share in SHARES)
+        return jnp.where(is_inner, mid, end)
 
     def round_cross(g):
         take(some(g, 1), got_sem.at[crossed, g])
 
-        @pl.when(crosses(g))
+        @pl.when(crosses(g, inner))
         def _():
             give(g, x_peer, rest, 1, frame_of(x_at, z_pair))
 
@@ -333,7 +334,7 @@
     def round_line(g):
         take(some(g, 2), got_sem.at[lined, g])
 
-        @pl.when(inner)
+        @pl.when(inner & (g >= DIRECT))
         def _():
             give(g, frame_of(x_at, z_end), lined, 1, frame_of(x_at, z_pair))
 
@@ -345,7 +346,7 @@
     def round_pair(g):
         take(some(g, 1), got_sem.at[paired, g])
 
-        @pl.when(jnp.logical_not(crosses(g)))
+        @pl.when(jnp.logical_not(crosses(g, jnp.logical_not(inner))))
         def _():
             give(g, frame_of(x_at, z_pair), rest, 0, x_peer)
 
@@ -386,11 +387,8 @@
 
     def arrival(j):
         slot = jnp.where(j == 0, 0, jnp.where(j == 1, slots - 1, j - 1))
+        slot = jnp.where(inner, slot, slots - 1 - j)
         return jnp.where(z_half == 0, slot, slots - 1 - slot)
-
-    def departure(j):
-        there = lax.rem(place + slots // 2 * (1 - j // 2), slots)
-        return jnp.where(lax.rem(j, 2) == 0, there + 1 - 2 * lax.rem(there, 2), there)
 
     def noisy_local():
         return pltpu.make_async_copy(noisy_ref.at[place, 0], n_ref.at[place], n_sem.at[0])
@@ -528,7 +526,7 @@
         build(xe, slot, e_recv[slot], columns(peer))
 
     def end_second(j):
-        slot = departure(j)
+        slot = arrival(j)
         acc_ref[slot] = second_sum(1, slot, every[-1:], True, acc_ref[slot])
         out = (e_mine[slot].astype(jnp.float32) + finished(1, slot)).astype(jnp.bfloat16)
         full = out.reshape(2, slab_rows, side, half)
@@ -632,20 +630,22 @@
 
     take(w_ref.at[pl.ds(0, taps), pl.ds(0, depth)], y_sem.at[per_section])
     def sent(link, count):
-        high = max(k for k in range(1, groups + 1) if count % k == 0)
-        take(w_ref.at[pl.ds(0, high * width), pl.ds(0, count // high * depth)], sent_sem.at[link])
-
-    crossings = sum(crossing)
-    sent(0, 3 * groups + groups - crossings)
+        rows = count * width * depth
+        fits = [k for k in range(1, 2 * taps + 1) if rows % (16 * k) == 0 and rows // k <= lanes]
+        take(w_ref.at[pl.ds(0, fits[0]), pl.ds(0, rows // fits[0])], sent_sem.at[link])
+
+    end_count, mid_count = (sum(g % den < num for g in range(groups)) for num, den in SHARES)
     sent(2, 2 * line * groups)
 
     @pl.when(inner)
     def _():
-        sent(1, 4 * groups + crossings)
+        sent(0, 4 * groups - end_count)
+        sent(1, 4 * groups - DIRECT + mid_count)
 
     @pl.when(jnp.logical_not(inner))
     def _():
-        sent(1, 2 * groups + crossings)
+        sent(0, 4 * groups - mid_count)
+        sent(1, 2 * groups + DIRECT + end_count)
 
 
 def on_device(noisy_clips, conv_first, conv_second, temporal):
@@ -663,7 +663,7 @@
     kind = jnp.bfloat16
     return pl.pallas_call(
         functools.partial(fused_kernel, frames),
-        out_shape=jax.ShapeDtypeStruct((clips, 1, side // 2, side, lanes), kind),
+        out_shape=pltpu.VMEM((clips, 1, side // 2, side, lanes), kind),
         in_specs=[pl.BlockSpec(memory_space=pl.ANY)] * 4,
         out_specs=vmem,
         scratch_shapes=[

time: 88.6 us -> 84.9 us (0.958)
  Pallas kernels: 86.6 us -> 83.9 us
  local copies, waits for them, and re-layouts: 1.87 us -> 0.8 us
    pallas_call x1, Pallas kernels: 86.6 us -> 83.9 us  [on_device(): pl.pallas_call(functools.partial(fused_kernel, frames), out_shape=pltpu.V...]
    unnamed x1, local copies, waits for them, and re-layouts: 1.87 us -> 0.8 us
where the time goes in v5:
time: 84.9 us; the launch traced here: 84.7 us
  Pallas kernels  83.9 us (99%)
    pallas_call x1, Pallas kernels, on_device(): pl.pallas_call(functools.partial(fused_kernel, frames), out_shape=pltpu.V...  83.9 us

profile of v5, /device:TPU:0, one launch (start us, length us, event | category | flops | bytes accessed | tf_op | source)
XLA Modules:
  0.0 84.7 jit_solution(14982574897117036671)
XLA Ops:
  0.0 83.9 %shard_map.46 = bf16[4,1,8,16,512]{4,3,2,1,0:T(8,128)(2,1)S(1)} custom-call(bf16[4,1,16,16,512]{4,3,2,1,0:T(8,128)(2,1)} %noisy_ref.1, bf16[1,9,32,512]{3,2,1,0:T(8,128)(2,1)} %first_ref.1, bf16[1,9,32,512]{3,2,1,0:T(8,128)(2,1)} %second_ref.1, bf16[1,3,32,512]{3,2,1,0:T(8,128)(2,1)} %time_ref.1), custom_call_target="tpu_custom_call" | custom-call | tf_op jit(solution)/shard_map/pallas_call | solution.py:664
  83.9 0.8 copy.6

commit v6 on v5

--- a/solution.py
+++ b/solution.py
@@ -136,39 +136,39 @@
 CODE, PACK, EVENTS = 16, 3, 127
 ORDERS = (
     (
-        6291712, 221442, 1126416, 3277873, 332339, 1253488, 406548, 464161,
-        4203061, 544822, 3613462, 8486977, 2392599, 623441, 5380162, 9539640,
-        9577795, 5449363, 723524, 2577433, 4536588, 10507578, 2639536, 10573338,
-        859057, 5750855, 3908124, 10693057, 12729416, 5817130, 2871325, 9722185,
-        9818429, 13773898, 2968470, 13851482, 6048919, 11838541, 10837472, 10936757,
-        11002609, 15983602, 240,
+        131328, 6292483, 3149921, 1192209, 1323539, 3416115, 2236784, 409605,
+        8397575, 8552784, 3507009, 541265, 5379364, 3544720, 3610513, 2462610,
+        1575235, 4466259, 11575352, 2577418, 4567457, 5576971, 4597922, 1718540,
+        3850326, 1784769, 10685767, 5720258, 1850563, 13642072, 4008477, 5851601,
+        9776020, 2937418, 13851286, 4926871, 6010020, 11904332, 5103708, 6137569,
+        14873072, 14938791, 243,
     ),
     (
-        6291712, 221442, 1126416, 3277873, 332339, 1253488, 3409428, 8486945,
-        8618517, 2230069, 3544640, 2295888, 1524023, 2361681, 5380162, 9539640,
-        9577795, 5449363, 11575321, 11641156, 742410, 2573730, 3757324, 3842886,
-        12604954, 4668353, 3981864, 5712323, 13638683, 13715469, 4794968, 1954365,
-        9802841, 9849387, 13851180, 11838615, 10832685, 5004213, 14703782, 14868813,
-        15837021, 15983602, 240,
+        24583, 155905, 1060867, 1126660, 1208370, 1315635, 2176032, 336448,
+        3493894, 8552832, 5325187, 541219, 1390390, 2396242, 9508630, 4428344,
+        3773193, 10507032, 10560944, 4466353, 2597386, 10703897, 5573445, 2624582,
+        12604954, 2736442, 870171, 12721211, 13653820, 2802504, 13712728, 1911625,
+        9722322, 9841813, 9950026, 4938285, 11838555, 14703692, 11904333, 15752673,
+        14872998, 14938791, 243,
     ),
     (
-        6291712, 221442, 2101520, 1180720, 340257, 3285616, 2295315, 4199475,
-        4280327, 1389604, 2426961, 8405557, 5379713, 4428176, 8533542, 1528722,
-        3642243, 599876, 676888, 4536360, 5615776, 2704907, 11641145, 4656214,
-        2767522, 1726233, 3916451, 4768555, 5770523, 13781308, 5844161, 4898966,
-        3002652, 5936445, 4954067, 9752605, 6048859, 5104294, 14919517, 15971749,
-        11838689, 15786226, 241,
+        131328, 1073504, 2101507, 266800, 7352609, 1258018, 1323811, 3417093,
+        8405312, 5276289, 426833, 5375810, 3510309, 1413443, 3548818, 5457043,
+        2561544, 1521492, 2666656, 10569016, 4609457, 1587465, 10619478, 4702219,
+        836259, 2705466, 1687895, 12802074, 3869994, 13769755, 3943379, 5886025,
+        4009108, 9837898, 13720215, 4953389, 5026980, 6071899, 5104352, 6141349,
+        15902689, 15986915, 241,
     ),
     (
-        6291712, 221442, 2101520, 1180720, 340257, 3285616, 2295315, 8393779,
-        8552768, 5244803, 3417153, 545045, 4338981, 9458198, 2507665, 9671222,
-        10491731, 2570160, 11641156, 5507352, 2662922, 10700088, 4590421, 5639225,
-        4702658, 12632873, 1710423, 866858, 13769544, 2825304, 4838203, 5848108,
-        4888470, 5936593, 1916205, 13650854, 5983380, 11904348, 5104353, 6153127,
-        11838707, 14742257, 240,
+        24583, 155905, 1114896, 7352352, 2167300, 2233137, 1323525, 8401699,
+        4261440, 8618625, 1397072, 4338724, 9458184, 9505091, 1455397, 9671191,
+        3548966, 4462647, 11575379, 11641113, 5519400, 5612101, 2704906, 5677881,
+        12782530, 12601100, 2802007, 1718797, 4837448, 3877720, 9722139, 9884188,
+        13712428, 4857237, 13843757, 4938391, 11838555, 14703692, 5104294, 15902557,
+        11904483, 14807283, 241,
     ),
 )
-DIRECT, SHARES = 0, ((1, 3), (2, 5))
+DIRECT, SHARES = 0, ((1, 3), (1, 4))
 
 
 def fused_kernel(
@@ -327,7 +327,7 @@
 
         @pl.when(crosses(g, inner))
         def _():
-            give(g, x_peer, rest, 1, frame_of(x_at, z_pair))
+            give(g, x_peer, rest, 3, frame_of(x_at, z_pair))
 
         give_core(g, x_peer)
 
@@ -348,7 +348,7 @@
 
         @pl.when(jnp.logical_not(crosses(g, jnp.logical_not(inner))))
         def _():
-            give(g, frame_of(x_at, z_pair), rest, 0, x_peer)
+            give(g, frame_of(x_at, z_pair), rest, 4, x_peer)
 
         give_core(g, frame_of(x_at, z_pair))
 
@@ -635,17 +635,20 @@
         take(w_ref.at[pl.ds(0, fits[0]), pl.ds(0, rows // fits[0])], sent_sem.at[link])
 
     end_count, mid_count = (sum(g % den < num for g in range(groups)) for num, den in SHARES)
+    sent(0, 3 * groups)
     sent(2, 2 * line * groups)
 
     @pl.when(inner)
     def _():
-        sent(0, 4 * groups - end_count)
-        sent(1, 4 * groups - DIRECT + mid_count)
+        sent(1, 4 * groups - DIRECT)
+        sent(3, mid_count)
+        sent(4, groups - end_count)
 
     @pl.when(jnp.logical_not(inner))
     def _():
-        sent(0, 4 * groups - mid_count)
-        sent(1, 2 * groups + DIRECT + end_count)
+        sent(1, 2 * groups + DIRECT)
+        sent(3, end_count)
+        sent(4, groups - mid_count)
 
 
 def on_device(noisy_clips, conv_first, conv_second, temporal):
@@ -683,7 +686,7 @@
             dma((5,)),
             dma((per_section + 1,)),
             dma((5, 2 * per_section)),
-            dma((3,)),
+            dma((5,)),
             dma((3, clips)),
             dma((2, 3)),
             dma((2, clips)),

time: 84.9 us -> 83.5 us (0.984)
  Pallas kernels: 83.9 us -> 82.6 us
    pallas_call x1, Pallas kernels: 83.9 us -> 82.6 us  [on_device(): pl.pallas_call(functools.partial(fused_kernel, frames), out_shape=pltpu.V...]
where the time goes in v6:
time: 83.5 us; the launch traced here: 83.4 us
  Pallas kernels  82.6 us (99%)
    pallas_call x1, Pallas kernels, on_device(): pl.pallas_call(functools.partial(fused_kernel, frames), out_shape=pltpu.V...  82.6 us

profile of v6, /device:TPU:0, one launch (start us, length us, event | category | flops | bytes accessed | tf_op | source)
XLA Modules:
  0.0 83.4 jit_solution(11842424044129867715)
XLA Ops:
  0.0 82.6 %shard_map.46 = bf16[4,1,8,16,512]{4,3,2,1,0:T(8,128)(2,1)S(1)} custom-call(bf16[4,1,16,16,512]{4,3,2,1,0:T(8,128)(2,1)} %noisy_ref.1, bf16[1,9,32,512]{3,2,1,0:T(8,128)(2,1)} %first_ref.1, bf16[1,9,32,512]{3,2,1,0:T(8,128)(2,1)} %second_ref.1, bf16[1,3,32,512]{3,2,1,0:T(8,128)(2,1)} %time_ref.1), custom_call_target="tpu_custom_call" | custom-call | tf_op jit(solution)/shard_map/pallas_call | solution.py:667
  82.6 0.8 copy.6

commit v7 on v6

--- a/solution.py
+++ b/solution.py
@@ -137,35 +137,35 @@
 ORDERS = (
     (
         131328, 6292483, 3149921, 1192209, 1323539, 3416115, 2236784, 409605,
-        8397575, 8552784, 3507009, 541265, 5379364, 3544720, 3610513, 2462610,
-        1575235, 4466259, 11575352, 2577418, 4567457, 5576971, 4597922, 1718540,
-        3850326, 1784769, 10685767, 5720258, 1850563, 13642072, 4008477, 5851601,
-        9776020, 2937418, 13851286, 4926871, 6010020, 11904332, 5103708, 6137569,
-        14873072, 14938791, 243,
+        8402183, 4292944, 8594306, 541265, 5379364, 3544720, 3610513, 2462610,
+        1575235, 4466259, 10500106, 3757232, 11641127, 1641285, 4629077, 2628108,
+        12697686, 870185, 1784483, 1850306, 3982167, 5777992, 13647177, 9722141,
+        9818411, 13781548, 5909910, 9950027, 10767451, 5070004, 10837472, 10936757,
+        15786737, 14938791, 243,
     ),
     (
-        24583, 155905, 1060867, 1126660, 1208370, 1315635, 2176032, 336448,
+        24583, 155905, 266243, 3215664, 1208370, 1315635, 2176032, 336448,
         3493894, 8552832, 5325187, 541219, 1390390, 2396242, 9508630, 4428344,
-        3773193, 10507032, 10560944, 4466353, 2597386, 10703897, 5573445, 2624582,
-        12604954, 2736442, 870171, 12721211, 13653820, 2802504, 13712728, 1911625,
-        9722322, 9841813, 9950026, 4938285, 11838555, 14703692, 11904333, 15752673,
-        14872998, 14938791, 243,
+        9648393, 10507032, 10596389, 4466353, 2597386, 10703897, 5573445, 2624582,
+        3823130, 4663744, 3870145, 5708827, 13647042, 2802504, 13719613, 13773641,
+        9722141, 2922133, 9950026, 10770989, 5983156, 5027237, 5103708, 14853857,
+        11006301, 15983602, 240,
     ),
     (
-        131328, 1073504, 2101507, 266800, 7352609, 1258018, 1323811, 3417093,
-        8405312, 5276289, 426833, 5375810, 3510309, 1413443, 3548818, 5457043,
-        2561544, 1521492, 2666656, 10569016, 4609457, 1587465, 10619478, 4702219,
-        836259, 2705466, 1687895, 12802074, 3869994, 13769755, 3943379, 5886025,
-        4009108, 9837898, 13720215, 4953389, 5026980, 6071899, 5104352, 6141349,
-        15902689, 15986915, 241,
+        131328, 1073504, 2101507, 266800, 7352609, 1258018, 3351301, 3417108,
+        8405312, 5276289, 8586833, 1378114, 3482962, 4428176, 3548818, 541843,
+        595539, 1521447, 11575380, 4536360, 11641173, 2693190, 1653078, 723618,
+        4694842, 5704898, 4729537, 5770688, 3877827, 1788186, 5886930, 3943574,
+        13670172, 2987082, 5905725, 4953553, 5004198, 10871388, 5104053, 14726308,
+        15902557, 15790563, 243,
     ),
     (
         24583, 155905, 1114896, 7352352, 2167300, 2233137, 1323525, 8401699,
         4261440, 8618625, 1397072, 4338724, 9458184, 9505091, 1455397, 9671191,
-        3548966, 4462647, 11575379, 11641113, 5519400, 5612101, 2704906, 5677881,
-        12782530, 12601100, 2802007, 1718797, 4837448, 3877720, 9722139, 9884188,
-        13712428, 4857237, 13843757, 4938391, 11838555, 14703692, 5104294, 15902557,
-        11904483, 14807283, 241,
+        3548966, 4462647, 11575379, 10572825, 3680433, 5612101, 2704906, 5677881,
+        12782530, 12601100, 2802007, 1718797, 5785928, 3877842, 9853211, 9818396,
+        1915948, 9752650, 5913901, 9915347, 10898523, 5104220, 6153127, 15905956,
+        10875104, 14807989, 241,
     ),
 )
 DIRECT, SHARES = 0, ((1, 3), (1, 4))

time: 83.5 us -> 82.8 us (level)
  no operation moved by 1% of the time
where the time goes in v7:
time: 82.8 us; the launch traced here: 82.7 us
  Pallas kernels  81.9 us (99%)
    pallas_call x1, Pallas kernels, on_device(): pl.pallas_call(functools.partial(fused_kernel, frames), out_shape=pltpu.V...  81.9 us

profile of v7, /device:TPU:0, one launch (start us, length us, event | category | flops | bytes accessed | tf_op | source)
XLA Modules:
  0.0 82.7 jit_solution(1566636019087101132)
XLA Ops:
  0.0 81.9 %shard_map.46 = bf16[4,1,8,16,512]{4,3,2,1,0:T(8,128)(2,1)S(1)} custom-call(bf16[4,1,16,16,512]{4,3,2,1,0:T(8,128)(2,1)} %noisy_ref.1, bf16[1,9,32,512]{3,2,1,0:T(8,128)(2,1)} %first_ref.1, bf16[1,9,32,512]{3,2,1,0:T(8,128)(2,1)} %second_ref.1, bf16[1,3,32,512]{3,2,1,0:T(8,128)(2,1)} %time_ref.1), custom_call_target="tpu_custom_call" | custom-call | tf_op jit(solution)/shard_map/pallas_call | solution.py:667
  81.9 0.8 copy.6

commit v8 on v7

--- a/solution.py
+++ b/solution.py
@@ -530,9 +530,9 @@
         acc_ref[slot] = second_sum(1, slot, every[-1:], True, acc_ref[slot])
         out = (e_mine[slot].astype(jnp.float32) + finished(1, slot)).astype(jnp.bfloat16)
         full = out.reshape(2, slab_rows, side, half)
-        for rows_at in range(2):
-            o_full[2 * slot + rows_at] = full[rows_at]
+        o_full[2 * slot + peer] = jnp.where(peer == 0, full[0], full[1])
         o_copy(slot, peer).start()
+        o_full[2 * slot + seg] = jnp.where(seg == 0, full[0], full[1])
 
         @pl.when(slot != place)
         def _():

time: 82.8 us -> 82.9 us (level)
  no operation moved by 1% of the time
where the time goes in v8:
time: 82.9 us; the launch traced here: 82.7 us
  Pallas kernels  81.9 us (99%)
    pallas_call x1, Pallas kernels, on_device(): pl.pallas_call(functools.partial(fused_kernel, frames), out_shape=pltpu.V...  81.9 us

profile of v8, /device:TPU:0, one launch (start us, length us, event | category | flops | bytes accessed | tf_op | source)
XLA Modules:
  0.0 82.7 jit_solution(10629257022419139045)
XLA Ops:
  0.0 81.9 %shard_map.46 = bf16[4,1,8,16,512]{4,3,2,1,0:T(8,128)(2,1)S(1)} custom-call(bf16[4,1,16,16,512]{4,3,2,1,0:T(8,128)(2,1)} %noisy_ref.1, bf16[1,9,32,512]{3,2,1,0:T(8,128)(2,1)} %first_ref.1, bf16[1,9,32,512]{3,2,1,0:T(8,128)(2,1)} %second_ref.1, bf16[1,3,32,512]{3,2,1,0:T(8,128)(2,1)} %time_ref.1), custom_call_target="tpu_custom_call" | custom-call | tf_op jit(solution)/shard_map/pallas_call | solution.py:667
  81.9 0.8 copy.6
